TPU v7x, 32 devices: a whole 2x2x4 slice. The times are simulated.
32 devices in a mesh: dp: 4 (over x, core), tensor: 8 (over z, y).
Axes of the slice: x: 2, y: 2, z: 4, core: 2. Of those that a mesh axis runs over, the one named last changes fastest.
Arguments:
- block_input: bfloat16 [6144, 2048], P(('dp', 'tensor')), may hold values from -6 to 6
- norm_gain: bfloat16 [2048], P('dp'), may hold values from 0.5 to 1.5
- in_weight: bfloat16 [2, 2048, 4096], P(None, 'dp', 'tensor'), may hold values from -0.125 to 0.125
- conv_weight: bfloat16 [4, 32, 128], P(None, 'tensor', 'dp'), may hold values from -0.5 to 0.5
- conv_bias: bfloat16 [32, 128], P('tensor', 'dp'), may hold values from -0.5 to 0.5
- select_weight: bfloat16 [32, 128, 160], P('tensor', 'dp'), may hold values from -0.09375 to 0.09375
- delta_weight: bfloat16 [128, 4096], P('dp', 'tensor'), may hold values from -0.5 to 0.5
- delta_bias: bfloat16 [32, 128], P('tensor', 'dp'), may hold values from -6 to -1
- decay_log: bfloat16 [4096, 16], P('tensor', 'dp'), may hold values from 0 to 2.765625
- skip_weight: bfloat16 [32, 128], P('tensor', 'dp'), may hold values from 0.5 to 1.5
- out_weight: bfloat16 [4096, 2048], P('tensor', 'dp'), may hold values from -0.1875 to 0.1875
- out_cotangent: bfloat16 [6144, 2048], P(('dp', 'tensor')), may hold values from -6 to 6
- seq_lengths: int32 [4, 4], P('dp'), may hold values from 1 to 1152, 1536 in all within a row
- deal_order: int32 [6144], P(('dp', 'tensor')), may hold values from 0 to 6143, as said below
Outputs:
- block_output: bfloat16 [6144, 2048], P(('dp', 'tensor'))
- input_grad: bfloat16 [6144, 2048], P(('dp', 'tensor'))
- norm_gain_grad: float32 [2048], P('dp')
- in_weight_grad: float32 [2, 2048, 4096], P(None, 'dp', 'tensor')
- conv_weight_grad: float32 [4, 32, 128], P(None, 'tensor', 'dp')
- conv_bias_grad: float32 [32, 128], P('tensor', 'dp')
- select_weight_grad: float32 [32, 128, 160], P('tensor', 'dp')
- delta_weight_grad: float32 [128, 4096], P('dp', 'tensor')
- delta_bias_grad: float32 [32, 128], P('tensor', 'dp')
- decay_log_grad: float32 [4096, 16], P('tensor', 'dp')
- skip_weight_grad: float32 [32, 128], P('tensor', 'dp')
- out_weight_grad: float32 [4096, 2048], P('tensor', 'dp')
Inputs may be any that keep to these rules, and one draw needn't show every extreme that they name: A permutation of the tokens: dealt place p holds the token of given place deal_order[p]. p and deal_order[p] lie in the same one of the 8 runs of 192 places inside their blocks of 1536 places, and each aligned run of 192 given places sends exactly 48 tokens to each block of 1536 dealt places. `seq_lengths`: each row sums to 1536; its largest entry is exactly 1152.
All inputs are finite; a program needn't handle non-finite values.
Results may differ from a plain program's by a relative error of at most 0.012.
Values may be sent and summed in bfloat16 or wider, within the bound.
No kernel may reach another device: no remote copies, remote signals or barrier semaphores. Data moves between devices by JAX's collectives and lax.ppermute only.
A program may use at most 320 MiB of HBM per device.

v0:
```python
import functools

import jax
import jax.numpy as jnp
from jax import lax
from jax.experimental import pallas as pl
from jax.experimental.pallas import tpu as pltpu
from jax.sharding import PartitionSpec as P

EPSILON = 1e-05
FAR = 1e30
LANES = 128
STEP = 48
SPAN = 16
SMALL = pl.CostEstimate(flops=1, transcendentals=0, bytes_accessed=1)
NT = (((1,), (1,)), ((), ()))
TN = (((0,), (0,)), ((), ()))
F32 = jnp.float32
BF16 = jnp.bfloat16


def softplus(v):
    return jnp.maximum(v, 0.0) + jnp.log1p(jnp.exp(-jnp.abs(v)))


def sigmoid(v):
    return 1.0 / (1.0 + jnp.exp(-v))


def mm(a, b, dims=(((1,), (0,)), ((), ()))):
    return lax.dot_general(a, b, dims, preferred_element_type=F32)


def column_at(states, tokens):
    return lax.broadcasted_iota(jnp.int32, (states, tokens), 1)


def write_packed(out_ref, low, wide_ref):
    rows, rank = low.shape
    states = wide_ref.shape[0] // 2
    rest = rows - LANES
    out_ref[0, 0:rows, :] = low.astype(out_ref.dtype)
    out_ref[0, rows:rows + 2 * states, :] = wide_ref[:, 0:LANES].astype(out_ref.dtype)
    tail = wide_ref[:, LANES:2 * LANES]
    lane = lax.broadcasted_iota(jnp.int32, (states, LANES), 1)
    both = jnp.where(lane < rest, tail[:states], pltpu.roll(tail[states:], rest, 1))
    out_ref[0, rows + 2 * states:rows + 3 * states, :] = both.astype(out_ref.dtype)


def read_packed(in_ref, states):
    rows = in_ref.shape[1] - 3 * states
    rest = rows - LANES
    low = in_ref[0, 0:rows, :]
    head = in_ref[0, rows:rows + 2 * states, :].astype(F32)
    both = in_ref[0, rows + 2 * states:rows + 3 * states, :].astype(F32)
    first = jnp.concatenate([head[:states], both], axis=1)
    second = jnp.concatenate([head[states:], pltpu.roll(both, LANES - rest, 1)], axis=1)
    return low, first, second


def front_kernel(me_ref, inner_ref, offset_ref, taps_ref, shift_ref, low_ref, bc_ref, act_ref, part_ref, ext_s, wide_s):
    rows = inner_ref.shape[0]
    taps = taps_ref.shape[0]

    @pl.when(pl.program_id(0) == 0)
    def _():
        ext_s[0:8, :] = jnp.zeros((8, ext_s.shape[1]), F32)

    ext_s[8:8 + rows, :] = inner_ref[...].astype(F32)
    offset = offset_ref[...]
    conv = shift_ref[...] + taps_ref[0:1, :] * ext_s[8:8 + rows, :]
    for k in range(1, taps):
        conv += jnp.where(offset >= k, taps_ref[k:k + 1, :], 0.0) * ext_s[pl.ds(8 - k, rows), :]
    act = (conv * sigmoid(conv)).astype(BF16)
    act_ref[...] = act
    ext_s[0:8, :] = ext_s[rows:rows + 8, :]
    wide_s[:, 0:rows] = mm(bc_ref[...], act, NT)
    write_packed(part_ref, mm(act, low_ref[...]), wide_s)


def front(me, projected, offset, taps, shift, low_w, bc_w):
    tokens, channels = projected.shape[0], taps.shape[1]
    runs, rows = tokens // ROWS[0], ROWS[0]
    packed = rows + 3 * bc_w.shape[0] // 2
    row = lambda i, me: (i, 0)
    fixed = lambda i, me: (0, 0)
    return pl.pallas_call(
        front_kernel,
        name="front",
        grid_spec=pltpu.PrefetchScalarGridSpec(
            num_scalar_prefetch=1,
            grid=(runs,),
            in_specs=[
                pl.BlockSpec((rows, channels), row),
                pl.BlockSpec((rows, 1), row),
                pl.BlockSpec(taps.shape, fixed),
                pl.BlockSpec(shift.shape, fixed),
                pl.BlockSpec(low_w.shape, fixed),
                pl.BlockSpec(bc_w.shape, fixed),
            ],
            out_specs=[pl.BlockSpec((rows, channels), row), pl.BlockSpec((1, packed, LANES), lambda i, me: (i ^ me[0], 0, 0))],
            scratch_shapes=[pltpu.VMEM((rows + 8, channels), F32), pltpu.VMEM((bc_w.shape[0], 2 * LANES), F32)],
        ),
        out_shape=[
            pltpu.HBM((tokens, channels), BF16),
            jax.ShapeDtypeStruct((runs, packed, LANES), BF16),
        ],
        compiler_params=pltpu.CompilerParams(dimension_semantics=("arbitrary",), vmem_limit_bytes=8 << 20),
        cost_estimate=SMALL,
    )(me, in_hbm(projected), offset, taps, shift, low_w, bc_w)


ROWS = [192]


def spread_mask(rows, states):
    width = SPAN * states
    row = lax.broadcasted_iota(jnp.int32, (rows, width), 0) % SPAN
    return row == lax.broadcasted_iota(jnp.int32, (rows, width), 1) // states


def tile_matrix(states):
    width = SPAN * states
    row = lax.broadcasted_iota(jnp.int32, (states, width), 0)
    return (row == lax.broadcasted_iota(jnp.int32, (states, width), 1) % states).astype(BF16)


def spread_columns(columns, rows, states):
    tiled = mm(columns[:, 0:rows].astype(BF16), tile_matrix(states), TN)
    return jnp.where(spread_mask(rows, states), tiled, 0.0).astype(BF16)


def forward_kernel(kept, me_ref, pack_ref, act_ref, gate_ref, offset_ref, dw_ref, bias_ref, rate_ref, skip_ref, h_in, *rest):
    pre_ref, y_ref, gated_ref, hist_ref, h_s, dtm_s, u_s = rest[kept:]
    states, channels = rate_ref.shape
    chunk = act_ref.shape[0]

    @pl.when(pl.program_id(0) == 0)
    def _():
        h_s[...] = h_in[...]

    low, bt, ct = read_packed(pack_ref, states)
    wide = bt.shape[1]
    pre = mm(low, dw_ref[...]) + bias_ref[...]
    pre_ref[...] = pre
    dt = softplus(pre)
    act = act_ref[...].astype(F32)
    u_s[...] = dt * act
    dtm_s[...] = jnp.where(offset_ref[...] == 0, FAR, dt)
    rate = rate_ref[...]

    def group(g, h):
        base = pl.multiple_of(g * STEP, STEP)
        bg = pltpu.roll(bt, wide - base, 1)
        dtm = dtm_s[pl.ds(base, STEP), :]
        u = u_s[pl.ds(base, STEP), :]
        for j in range(STEP):
            a = jnp.exp(dtm[j:j + 1, :] * rate)
            h = a * h + u[j:j + 1, :] * bg[:, j:j + 1]
            at = pl.multiple_of((base + j) * states, states)
            hist_ref[pl.ds(at, states), :] = h.astype(BF16)
        return h

    h_s[...] = lax.fori_loop(0, chunk // STEP, group, h_s[...])
    spread = spread_columns(ct, chunk, states)
    width = SPAN * states
    for g in range(chunk // SPAN):
        rows = slice(g * SPAN, (g + 1) * SPAN)
        y_ref[rows, :] = mm(spread[rows, :], hist_ref[g * width:(g + 1) * width, :])
    y = y_ref[...] + skip_ref[...] * act
    y_ref[...] = y
    gate = gate_ref[...].astype(F32)
    gated_ref[...] = (y * gate * sigmoid(gate)).astype(BF16)


def scan_forward(me, pack, act, projected, offset, delta_w, bias, rate, skip, held, whole, first, steps):
    tokens, channels = act.shape
    states = rate.shape[0]
    chunk = ROWS[0]
    row = lambda i, me: (first + i, 0)
    fixed = lambda i, me: (0, 0)
    done = steps * chunk
    return pl.pallas_call(
        functools.partial(forward_kernel, len(whole)),
        name="scan_forward",
        grid_spec=pltpu.PrefetchScalarGridSpec(
            num_scalar_prefetch=1,
            grid=(steps,),
            in_specs=[
                pl.BlockSpec((1,) + pack.shape[1:], lambda i, me: ((first + i) ^ me[0], 0, 0)),
                pl.BlockSpec((chunk, channels), row),
                pl.BlockSpec((chunk, channels), lambda i, me: (first + i, 1)),
                pl.BlockSpec((chunk, 1), row),
                pl.BlockSpec(delta_w.shape, fixed),
                pl.BlockSpec(bias.shape, fixed),
                pl.BlockSpec(rate.shape, fixed),
                pl.BlockSpec(skip.shape, fixed),
                pl.BlockSpec(rate.shape, fixed),
            ] + [pl.BlockSpec(memory_space=pl.ANY)] * len(whole),
            out_specs=[
                pl.BlockSpec((chunk, channels), row),
                pl.BlockSpec((chunk, channels), row),
                pl.BlockSpec((chunk, channels), row),
                pl.BlockSpec((chunk * states, channels), row),
                pl.BlockSpec(rate.shape, fixed),
            ],
            scratch_shapes=[
                pltpu.VMEM((chunk, channels), F32),
                pltpu.VMEM((chunk, channels), F32),
            ],
        ),
        out_shape=[
            pltpu.HBM((tokens, channels), F32),
            pltpu.HBM((tokens, channels), F32),
            pltpu.HBM((tokens, channels), BF16),
            pltpu.HBM((tokens * states, channels), BF16),
            jax.ShapeDtypeStruct(rate.shape, F32),
        ],
        input_output_aliases={10 + i: i for i in range(len(whole))},
        compiler_params=pltpu.CompilerParams(dimension_semantics=("arbitrary",), vmem_limit_bytes=16 << 20),
        cost_estimate=SMALL,
    )(me, pack, in_hbm(act), in_hbm(projected), offset, delta_w, bias, rate, skip, held, *(in_hbm(v) for v in whole))


def backward_kernel(kept, me_ref, pack_ref, pre_ref, act_ref, gate_ref, gg_ref, y_ref, offset_ref,
                    hist_ref, prior_ref, dw_ref, rate_ref, skip_ref, carry_in, rgrad_in, dwgrad_in, rows_in, *rest):
    (ggate_ref, gact_ref, part_ref, carry_s, rgrad_ref, dwgrad_ref, rows_ref,
     dtm_s, u_s, dt_s, gy_s, drive_s, decay_s, wide_s, adj_s, thr_s) = rest[kept:]
    states, channels = rate_ref.shape
    chunk = act_ref.shape[0]

    @pl.when(pl.program_id(0) == 0)
    def _():
        carry_s[...] = carry_in[...]
        rgrad_ref[...] = rgrad_in[...]
        dwgrad_ref[...] = dwgrad_in[...]
        rows_ref[...] = rows_in[...]

    low, bt, ct = read_packed(pack_ref, states)
    wide = bt.shape[1]
    pre = pre_ref[...]
    dt = softplus(pre)
    act = act_ref[...].astype(F32)
    dt_s[...] = dt
    u_s[...] = dt * act
    dtm_s[...] = jnp.where(offset_ref[...] == 0, FAR, dt)
    gate = gate_ref[...].astype(F32)
    sig = sigmoid(gate)
    gg = gg_ref[...].astype(F32) * sig
    gy = gg * gate
    gy_s[...] = gy
    ggate_ref[...] = (gg * y_ref[...] * (1.0 + gate * (1.0 - sig))).astype(BF16)
    rate = rate_ref[...]
    groups = chunk // STEP

    def group(k, held):
        carry, rgrad = held
        g = groups - 1 - k
        base = pl.multiple_of(g * STEP, STEP)
        cg = pltpu.roll(ct, wide - base, 1)
        dtm = dtm_s[pl.ds(base, STEP), :]
        dts = dt_s[pl.ds(base, STEP), :]
        gys = gy_s[pl.ds(base, STEP), :]
        for j in reversed(range(STEP)):
            if j > 0:
                at = pl.multiple_of((base + j - 1) * states, states)
                prior = hist_ref[pl.ds(at, states), :].astype(F32)
            else:
                at = pl.multiple_of(jnp.maximum(base - 1, 0) * states, states)
                prior = jnp.where(base == 0, prior_ref[...], hist_ref[pl.ds(at, states), :]).astype(F32)
            a = jnp.exp(dtm[j:j + 1, :] * rate)
            adj = cg[:, j:j + 1] * gys[j:j + 1, :] + carry
            carry = a * adj
            through = carry * prior
            rgrad = rgrad + through * dts[j:j + 1, :]
            at = pl.multiple_of((base + j) * states, states)
            adj_s[pl.ds(at, states), :] = adj.astype(BF16)
            thr_s[pl.ds(at, states), :] = (through * rate).astype(BF16)
        return carry, rgrad

    carry, rgrad = lax.fori_loop(0, groups, group, (carry_s[...], rgrad_ref[...]))
    carry_s[...] = carry
    rgrad_ref[...] = rgrad
    spread = spread_columns(bt, chunk, states)
    ones = jnp.where(spread_mask(SPAN, states), 1.0, 0.0).astype(BF16)
    width = SPAN * states
    ub = u_s[...].astype(BF16)
    gyb = gy.astype(BF16)
    ahead = (lax.broadcasted_iota(jnp.int32, (width, chunk), 1)
             - lax.broadcasted_iota(jnp.int32, (width, chunk), 0) // states)
    gb_all = jnp.zeros((width, chunk), F32)
    gc_all = jnp.zeros((width, chunk), F32)
    for g in range(chunk // SPAN):
        rows = slice(g * SPAN, (g + 1) * SPAN)
        adj = adj_s[g * width:(g + 1) * width, :]
        drive_s[rows, :] = mm(spread[rows, :], adj)
        decay_s[rows, :] = mm(ones, thr_s[g * width:(g + 1) * width, :])
        gb_all = jnp.where(ahead == g * SPAN, mm(adj, ub, NT), gb_all)
        gc_all = jnp.where(ahead == g * SPAN, mm(hist_ref[g * width:(g + 1) * width, :], gyb, NT), gc_all)
    tiles = tile_matrix(states)
    wide_s[0:states, 0:chunk] = mm(tiles, gb_all.astype(BF16))
    wide_s[states:2 * states, 0:chunk] = mm(tiles, gc_all.astype(BF16))
    drive = drive_s[...]
    gact_ref[...] = drive * dt + gy * skip_ref[...]
    gpre = ((drive * act + decay_s[...]) * sigmoid(pre)).astype(BF16)
    rows_ref[0:1, :] += jnp.sum(gy * act, axis=0, keepdims=True)
    rows_ref[1:2, :] += jnp.sum(gpre.astype(F32), axis=0, keepdims=True)
    dwgrad_ref[...] += mm(low, gpre, TN)
    write_packed(part_ref, mm(gpre, dw_ref[...], NT), wide_s)


def scan_backward(me, pack, pre, act, projected, gg, y, offset, hist, delta_w, rate, skip, held, whole, last, steps):
    tokens, channels = act.shape
    states = rate.shape[0]
    chunk = ROWS[0]
    row = lambda i, me: (last - i, 0)
    second = lambda i, me: (last - i, 1)
    run = lambda i, me: ((last - i) ^ me[0], 0, 0)
    fixed = lambda i, me: (0, 0)
    blocks = [pl.BlockSpec((chunk, channels), second), pl.BlockSpec((chunk, channels), row), pl.BlockSpec((1,) + pack.shape[1:], run)]
    shapes = [
        pltpu.HBM((tokens, 2 * channels), BF16),
        pltpu.HBM((tokens, channels), F32),
        jax.ShapeDtypeStruct(pack.shape, BF16),
    ]
    sums = [pl.BlockSpec(v.shape, fixed) for v in held]
    done = steps * chunk
    return pl.pallas_call(
        functools.partial(backward_kernel, len(whole)),
        name="scan_backward",
        grid_spec=pltpu.PrefetchScalarGridSpec(
            num_scalar_prefetch=1,
            grid=(steps,),
            in_specs=[
                pl.BlockSpec((1,) + pack.shape[1:], run),
                pl.BlockSpec((chunk, channels), row),
                pl.BlockSpec((chunk, channels), row),
                pl.BlockSpec((chunk, channels), second),
                pl.BlockSpec((chunk, channels), row),
                pl.BlockSpec((chunk, channels), row),
                pl.BlockSpec((chunk, 1), row),
                pl.BlockSpec((chunk * states, channels), row),
                pl.BlockSpec((states, channels), lambda i, me: (jnp.maximum((last - i) * chunk - 1, 0), 0)),
                pl.BlockSpec(delta_w.shape, fixed),
                pl.BlockSpec(rate.shape, fixed),
                pl.BlockSpec(skip.shape, fixed),
            ] + sums + [pl.BlockSpec(memory_space=pl.ANY)] * len(whole),
            out_specs=blocks + sums,
            scratch_shapes=[pltpu.VMEM((chunk, channels), F32)] * 6
            + [pltpu.VMEM((2 * states, 2 * LANES), F32)]
            + [pltpu.VMEM((chunk * states, channels), BF16)] * 2,
        ),
        out_shape=shapes + [jax.ShapeDtypeStruct(v.shape, F32) for v in held],
        input_output_aliases={17 + i: i for i in range(len(whole))},
        compiler_params=pltpu.CompilerParams(dimension_semantics=("arbitrary",), vmem_limit_bytes=24 << 20),
        cost_estimate=SMALL,
    )(me, pack, in_hbm(pre), in_hbm(act), in_hbm(projected), in_hbm(gg), in_hbm(y), offset, in_hbm(hist), in_hbm(hist), delta_w, rate, skip, *held, *(in_hbm(v) if k == 1 else v for k, v in enumerate(whole)))


def end_kernel(me_ref, pack_ref, gact_ref, act_ref, inner_ref, prior_ref, offset_ref, taps_ref, shift_ref, low_ref, bc_ref, grad_ref,
               ginner_ref, tapg_ref, selow_ref, selbc_ref, ext_s, after_s, wide_s):
    rows, channels = inner_ref.shape
    taps = taps_ref.shape[0]
    states = bc_ref.shape[0] // 2

    @pl.when(pl.program_id(0) == 0)
    def _():
        after_s[...] = jnp.zeros_like(after_s)
        tapg_ref[...] = jnp.zeros_like(tapg_ref)
        selow_ref[...] = jnp.zeros_like(selow_ref)
        selbc_ref[...] = jnp.zeros_like(selbc_ref)

    low, gbt, gct = read_packed(pack_ref, states)
    wide_s[0:states, :] = gbt
    wide_s[states:2 * states, :] = gct
    gbc = wide_s[:, 0:rows].astype(BF16)
    act = act_ref[...]
    selow_ref[...] += mm(act, low, TN)
    selbc_ref[...] += mm(gbc, act)
    gact = gact_ref[...] + mm(low, low_ref[...], NT) + mm(gbc, bc_ref[...], TN)
    before = prior_ref.shape[0]
    ext_s[0:before, :] = prior_ref[...].astype(F32)
    ext_s[before:before + rows, :] = inner_ref[...].astype(F32)
    offset = offset_ref[...]
    conv = shift_ref[...] + taps_ref[0:1, :] * ext_s[before:before + rows, :]
    for k in range(1, taps):
        conv += jnp.where(offset >= k, taps_ref[k:k + 1, :], 0.0) * ext_s[pl.ds(before - k, rows), :]
    q = sigmoid(conv)
    gconv = gact * q * (1.0 + conv * (1.0 - q))
    tapg_ref[taps:taps + 1, :] += jnp.sum(gconv, axis=0, keepdims=True)
    tapg_ref[0:1, :] += jnp.sum(gconv * ext_s[before:before + rows, :], axis=0, keepdims=True)
    ginner = gconv * taps_ref[0:1, :]
    for k in range(1, taps):
        masked = jnp.where(offset >= k, gconv, 0.0)
        tapg_ref[k:k + 1, :] += jnp.sum(masked * ext_s[pl.ds(before - k, rows), :], axis=0, keepdims=True)
        after_s[k - 1, rows:rows + 8, :] = after_s[k - 1, 0:8, :]
        after_s[k - 1, 0:rows, :] = masked * taps_ref[k:k + 1, :]
        ginner += after_s[k - 1, pl.ds(k, rows), :]
    ginner_ref[...] = ginner.astype(BF16)


def end(me, pack, gact, act, projected, offset, taps, shift, low_w, bc_w, grad_projected):
    tokens, channels = act.shape
    rows = ROWS[0]
    steps = tokens // rows
    row = lambda i, me: (steps - 1 - i, 0)
    fixed = lambda i, me: (0, 0)
    return pl.pallas_call(
        end_kernel,
        name="end",
        grid_spec=pltpu.PrefetchScalarGridSpec(
            num_scalar_prefetch=1,
            grid=(steps,),
            in_specs=[
                pl.BlockSpec((1,) + pack.shape[1:], lambda i, me: ((steps - 1 - i) ^ me[0], 0, 0)),
                pl.BlockSpec((rows, channels), row),
                pl.BlockSpec((rows, channels), row),
                pl.BlockSpec((rows, channels), row),
                pl.BlockSpec((16, channels), lambda i, me: (jnp.maximum((steps - 1 - i) * (rows // 16) - 1, 0), 0)),
                pl.BlockSpec((rows, 1), row),
                pl.BlockSpec(taps.shape, fixed),
                pl.BlockSpec(shift.shape, fixed),
                pl.BlockSpec(low_w.shape, fixed),
                pl.BlockSpec(bc_w.shape, fixed),
                pl.BlockSpec(memory_space=pl.ANY),
            ],
            out_specs=[
                pl.BlockSpec((rows, channels), row),
                pl.BlockSpec((8, channels), fixed),
                pl.BlockSpec(low_w.shape, fixed),
                pl.BlockSpec(bc_w.shape, fixed),
            ],
            scratch_shapes=[
                pltpu.VMEM((rows + 16, channels), F32),
                pltpu.VMEM((3, rows + 8, channels), F32),
                pltpu.VMEM((bc_w.shape[0], 2 * LANES), F32),
            ],
        ),
        out_shape=[
            pltpu.HBM(grad_projected.shape, BF16),
            jax.ShapeDtypeStruct((8, channels), F32),
            jax.ShapeDtypeStruct(low_w.shape, F32),
            jax.ShapeDtypeStruct(bc_w.shape, F32),
        ],
        input_output_aliases={11: 0},
        compiler_params=pltpu.CompilerParams(dimension_semantics=("arbitrary",), vmem_limit_bytes=14 << 20),
        cost_estimate=SMALL,
    )(me, pack, in_hbm(gact), in_hbm(act), in_hbm(projected), in_hbm(projected), offset, taps, shift, low_w, bc_w, in_hbm(grad_projected))


def weight_grad_kernel(count, turned, table_ref, *refs):
    a_refs, b_refs = refs[:count], refs[count:2 * count]
    out_ref, a_s, b_s = refs[-3:]
    rows = a_refs[0].shape[0]
    for s in range(count):
        a_s[s * rows:(s + 1) * rows, :] = a_refs[s][...]

    @pl.when(pl.program_id(0) == 0)
    def _():
        for s in range(count):
            b_s[s * rows:(s + 1) * rows, :] = b_refs[s][...]

    first, second = (b_s, a_s) if turned else (a_s, b_s)
    out_ref[0] = mm(first[...], second[...], TN).astype(BF16)


def weight_grad(table, distances, shards, b, column, channels, size, turned, slots=1, slot=0, into=()):
    rows, width = shards[0].shape
    block = width // size
    count = len(shards)
    shape = (1, channels, block) if turned else (1, block, channels)
    if distances is None:
        b_specs = [pl.BlockSpec((rows, channels), lambda i, table: (0, column))]
    else:
        b_specs = [pl.BlockSpec((rows, channels), lambda i, table, d=d: (table[d], column)) for d in distances]
    return pl.pallas_call(
        functools.partial(weight_grad_kernel, count, turned),
        name="weight_grad",
        grid_spec=pltpu.PrefetchScalarGridSpec(
            num_scalar_prefetch=1,
            grid=(size,),
            in_specs=[pl.BlockSpec((rows, block), lambda i, table: (0, i))] * count
            + b_specs + [pl.BlockSpec(memory_space=pl.ANY)] * len(into),
            out_specs=pl.BlockSpec(shape, lambda i, table: (i, slot, 0)),
            scratch_shapes=[pltpu.VMEM((rows * count, block), BF16), pltpu.VMEM((rows * count, channels), BF16)],
        ),
        out_shape=pltpu.HBM((size, slots * shape[1], shape[2]), BF16),
        input_output_aliases={1 + 2 * count + k: k for k in range(len(into))},
        compiler_params=pltpu.CompilerParams(dimension_semantics=("arbitrary",), vmem_limit_bytes=16 << 20),
        cost_estimate=SMALL,
    )(table, *(in_hbm(v) for v in shards), *([in_hbm(b)] * count), *(in_hbm(v) for v in into))


def weight_block(weight, dims, blocks):
    if dims[0][1] == (0,):
        columns = weight.shape[1] // blocks
        return pl.BlockSpec((weight.shape[0], columns), lambda i, *rest: (0, i)), columns
    columns = weight.shape[0] // blocks
    return pl.BlockSpec((columns, weight.shape[1]), lambda i, *rest: (i, 0)), columns


def placed_kernel(dims, count, table_ref, *refs):
    w_ref, out_ref = refs[count], refs[-1]
    for s in range(count):
        @pl.when(pl.program_id(1) == s)
        def _(s=s):
            out_ref[...] = mm(refs[s][...], w_ref[...], dims).astype(out_ref.dtype)


def pick_entry(values, i):
    chosen = values[0]
    for k in range(1, len(values)):
        chosen = jnp.where(i == k, values[k], chosen)
    return chosen


def placed_product(table, distances, shards, weight, dims, out):
    rows, width = shards[0].shape
    count, blocks = len(shards), 2
    spec, columns = weight_block(weight, dims, blocks)
    return pl.pallas_call(
        functools.partial(placed_kernel, dims, count),
        name="placed_product",
        grid_spec=pltpu.PrefetchScalarGridSpec(
            num_scalar_prefetch=1,
            grid=(blocks, count),
            in_specs=[pl.BlockSpec((rows, width), lambda i, k, table: (0, 0))] * count
            + [spec, pl.BlockSpec(memory_space=pl.ANY)],
            out_specs=pl.BlockSpec((rows, columns), lambda i, k, table: (pick_entry([table[d] for d in distances], k), i)),
        ),
        out_shape=pltpu.HBM(out.shape, out.dtype),
        input_output_aliases={count + 2: 0},
        compiler_params=pltpu.CompilerParams(dimension_semantics=("arbitrary", "arbitrary"), vmem_limit_bytes=16 << 20),
        cost_estimate=SMALL,
    )(table, *(in_hbm(v) for v in shards), in_hbm(weight), in_hbm(out))


def placed_halves_kernel(cuts, table_ref, first_ref, second_ref, *refs):
    w_refs, out_ref = refs[:cuts], refs[-1]
    depth = w_refs[0].shape[0]
    each = first_ref.shape[1] // depth
    total = None
    for c in range(cuts):
        ref, at = (first_ref, c) if c < each else (second_ref, c - each)
        term = mm(ref[:, at * depth:(at + 1) * depth], w_refs[c][...])
        total = term if total is None else total + term
    out_ref[...] = total.astype(out_ref.dtype)


def placed_halves(table, distance, first, second, weight, out):
    rows, middle = first.shape
    cuts = 8
    depth, width = weight.shape[0] // cuts, weight.shape[1]
    return pl.pallas_call(
        functools.partial(placed_halves_kernel, cuts),
        name="placed_halves",
        grid_spec=pltpu.PrefetchScalarGridSpec(
            num_scalar_prefetch=1,
            grid=(1,),
            in_specs=[pl.BlockSpec((rows, middle), lambda i, table: (0, 0))] * 2
            + [pl.BlockSpec((depth, width), lambda i, table, c=c: (c, 0)) for c in range(cuts)]
            + [pl.BlockSpec(memory_space=pl.ANY)],
            out_specs=pl.BlockSpec((rows, width), lambda i, table: (table[distance], 0)),
        ),
        out_shape=pltpu.HBM(out.shape, out.dtype),
        input_output_aliases={3 + cuts: 0},
        compiler_params=pltpu.CompilerParams(dimension_semantics=("arbitrary",), vmem_limit_bytes=16 << 20),
        cost_estimate=SMALL,
    )(table, in_hbm(first), in_hbm(second), *([in_hbm(weight)] * cuts), in_hbm(out))


def in_hbm(value):
    return pltpu.with_memory_space_constraint(value, pltpu.HBM)


def far_kernel(cuts, table_ref, g_ref, t_ref, *refs):
    w_refs, (ahead_ref, behind_ref) = refs[:cuts], refs[cuts:]
    columns = w_refs[0].shape[0]
    for ref, first in ((ahead_ref, True), (behind_ref, False)):
        @pl.when((pl.program_id(0) == 0) == first)
        def _(ref=ref):
            for c in range(cuts):
                at = slice(c * columns, (c + 1) * columns)
                ref[:, at] = (mm(g_ref[...], w_refs[c][...], NT) + t_ref[:, at].astype(F32)).astype(BF16)


def pair_kernel(cuts, table_ref, ga_ref, gb_ref, ta_ref, tb_ref, *refs, halves=False):
    w_refs, (ra_ref, rb_ref, ahead_ref, behind_ref) = refs[:cuts], refs[cuts:]
    rows, columns = ga_ref.shape[0], w_refs[0].shape[0]
    both = jnp.concatenate([ga_ref[...], gb_ref[...]], axis=0)
    low = pl.program_id(0) == 0
    for c in range(cuts):
        at = slice(c * columns, (c + 1) * columns)
        total = mm(both, w_refs[c][...], NT)
        ra, rb = ra_ref[:, at].astype(F32), rb_ref[:, at].astype(F32)
        if halves:
            ra, rb = jnp.where(low, ra, 0.0), jnp.where(low, 0.0, rb)
        ahead_ref[:, at] = (total[:rows] + ta_ref[:, at].astype(F32) + ra).astype(BF16)
        behind_ref[:, at] = (total[rows:] + tb_ref[:, at].astype(F32) + rb).astype(BF16)


def own_kernel(cuts, table_ref, g_ref, t_ref, *refs):
    w_refs, (ra_ref, rb_ref, place_ref, out_ref) = refs[:cuts], refs[cuts:]
    columns = w_refs[0].shape[0]
    for c in range(cuts):
        at = slice(c * columns, (c + 1) * columns)
        total = mm(g_ref[...], w_refs[c][...], NT) + t_ref[:, at].astype(F32)
        total = total + ra_ref[:, at].astype(F32) + rb_ref[:, at].astype(F32)
        out_ref[:, at] = mm(place_ref[...], total.astype(BF16)).astype(BF16)


def ring_step(kernel, table, distances, grads, terms, weight, arrived=(), place=None):
    rows, cuts = ROWS[0], 4
    width, channels = weight.shape[0], weight.shape[1] // 2
    half, columns = width // 2, width // (2 * cuts)
    fixed = lambda i, table: (0, 0)
    side = lambda i, table: (0, i)
    far = not arrived
    if far:
        outs, shape = [fixed, fixed], (rows, half)
    else:
        outs, shape = [side, side] if place is None else [side], (rows, width)
    small = not far and arrived[0].shape[1] == half
    extra = [] if place is None else [place]
    return pl.pallas_call(
        functools.partial(kernel, cuts, halves=True) if small else functools.partial(kernel, cuts),
        name=kernel.__name__,
        grid_spec=pltpu.PrefetchScalarGridSpec(
            num_scalar_prefetch=1,
            grid=(2,),
            in_specs=[pl.BlockSpec((rows, channels), lambda i, table, d=d: (table[d], 0)) for d in distances]
            + [pl.BlockSpec((rows, half), lambda i, table, d=d: (table[d], i)) for d in distances]
            + [pl.BlockSpec((columns, channels), lambda i, table, c=c: (i * cuts + c, 0)) for c in range(cuts)]
            + [pl.BlockSpec((rows, half), fixed if small else side) for v in arrived]
            + [pl.BlockSpec(v.shape, fixed) for v in extra],
            out_specs=[pl.BlockSpec((rows, half), m) for m in outs],
        ),
        out_shape=[pltpu.HBM(shape, BF16) for m in outs],
        compiler_params=pltpu.CompilerParams(dimension_semantics=("arbitrary",), vmem_limit_bytes=24 << 20),
        cost_estimate=SMALL,
    )(table, *([in_hbm(grads)] * len(distances)), *([in_hbm(terms)] * len(distances)), *([in_hbm(weight)] * cuts),
      *(in_hbm(v) for v in arrived), *extra)


def blank(*shapes):
    hbm = pl.BlockSpec(memory_space=pl.ANY)
    return pl.pallas_call(
        lambda *refs: None, name="blank", out_specs=[hbm] * len(shapes),
        out_shape=[pltpu.HBM(*v) for v in shapes],
        cost_estimate=SMALL)()


def deal_kernel(x_ref, cot_ref, order_ref, gain_ref, me_ref, sendx_ref, sendc_ref, pick_ref, place_ref):
    rows = x_ref.shape[0]
    dp_size = order_ref.shape[0]
    me = me_ref[0]
    group_tokens = me_ref[1]
    pair = rows // dp_size
    order = order_ref[...].astype(jnp.int32)
    near = lax.broadcasted_iota(jnp.int32, (dp_size, rows), 0)
    other = near ^ me
    source = order // group_tokens
    local = order % rows
    before = (
        lax.broadcasted_iota(jnp.int32, (rows, rows), 0) < lax.broadcasted_iota(jnp.int32, (rows, rows), 1)
    ).astype(BF16)
    slots = lax.broadcasted_iota(jnp.int32, (rows, rows), 0)
    chosen = source == me
    rank = mm(chosen.astype(BF16), before).astype(jnp.int32)
    slot = jnp.where(chosen, near * pair + rank, -1)
    pick = jnp.zeros((rows, rows), F32)
    for d in range(dp_size):
        pick += mm((slots == slot[d:d + 1, :]).astype(BF16), (slots == local[d:d + 1, :]).astype(BF16), NT)
    pick = pick.astype(BF16)
    pick_ref[...] = pick
    mine = source[0:1, :]
    held = (mine == other).astype(BF16)
    ranks = mm(held, before).astype(jnp.int32)
    arrived = jnp.sum(jnp.where(mine == other, near * pair + ranks, 0), axis=0, keepdims=True)
    place_ref[...] = (slots == arrived).astype(BF16)
    x = x_ref[...].astype(F32)
    rinv = lax.rsqrt(jnp.mean(x * x, axis=1, keepdims=True) + EPSILON)
    normed = (x * rinv * gain_ref[...]).astype(BF16)
    sendx_ref[...] = mm(pick, normed).astype(BF16)
    sendc_ref[...] = mm(pick, cot_ref[...]).astype(BF16)


def deal(x, cot, order, gain, me):
    rows, width = x.shape
    vm = pl.BlockSpec(memory_space=pltpu.VMEM)
    return pl.pallas_call(
        deal_kernel,
        name="deal",
        in_specs=[vm, vm, vm, vm, pl.BlockSpec(memory_space=pltpu.SMEM)],
        out_specs=[vm] * 4,
        out_shape=[
            jax.ShapeDtypeStruct((rows, width), BF16),
            jax.ShapeDtypeStruct((rows, width), BF16),
            jax.ShapeDtypeStruct((rows, rows), BF16),
            jax.ShapeDtypeStruct((rows, rows), BF16),
        ],
        compiler_params=pltpu.CompilerParams(vmem_limit_bytes=32 << 20),
        cost_estimate=SMALL,
    )(x, cot, order, gain, me)


def round_dot(a, b, dims=(((1,), (0,)), ((), ()))):
    return mm(a, b, dims).astype(BF16)


def after(value, *earlier):
    return lax.optimization_barrier((value,) + earlier)[0]


def flip(value, axis, bit):
    return lax.ppermute(value, axis, [(i, i ^ bit) for i in range(lax.axis_size(axis))])


def exchange(pieces, axis, stack=True):
    pieces = [pieces[0]] + [flip(pieces[d], axis, d) for d in range(1, lax.axis_size(axis))]
    return jnp.stack(pieces) if stack else pieces


def swap(values, axis):
    return lax.all_to_all(values, axis, split_axis=0, concat_axis=0, tiled=True)


def share(value, axis):
    return exchange([value] * lax.axis_size(axis), axis)


def in_order(pieces, axis):
    size, me, bit = lax.axis_size(axis), lax.axis_index(axis), 1
    while bit < size:
        split = pieces.reshape((size // (2 * bit), 2, bit) + pieces.shape[1:])
        turned = jnp.concatenate([split[:, 1:], split[:, :1]], axis=1)
        pieces = jnp.where((me // bit) % 2 == 1, turned, split).reshape(pieces.shape)
        bit *= 2
    return pieces


def cube_sum(value, axis, bit, end_bit):
    while bit < end_bit:
        value = value + flip(value, axis, bit)
        bit *= 2
    return value


class Bag(dict):
    def meet(self, values, *names):
        values, held = lax.optimization_barrier((values, {n: self[n] for n in names}))
        self.update(held)
        return values


def add_up(pieces):
    return jnp.sum(pieces.astype(F32), axis=0)


class Ring:
    def __init__(self, axis):
        self.axis = axis
        self.size = size = lax.axis_size(axis)
        columns = max(c for c in range(1, size) if size % c == 0 and c * c <= size)
        rows = size // columns
        cycle = [(0, c) for c in range(columns)]
        for r in range(1, rows):
            snake = range(1, columns)
            cycle += [(r, c) for c in (snake if r % 2 == 0 else reversed(snake))]
        cycle += [(r, 0) for r in reversed(range(1, rows))]
        order = [r * columns + c for r, c in cycle]
        place = {t: i for i, t in enumerate(order)}
        table = jnp.array([[order[(place[t] + d) % size] for d in range(size)] for t in range(size)], jnp.int32)
        self.at = lax.dynamic_index_in_dim(table, lax.axis_index(axis), 0, keepdims=False)
        self.forward = [(order[i], order[(i + 1) % size]) for i in range(size)]
        self.backward = [(b, a) for a, b in self.forward]

    def hop(self, value, ahead):
        return lax.ppermute(value, self.axis, self.forward if ahead else self.backward)


def ring_gather(ring, own, between):
    half, size = ring.size // 2, ring.size
    middle = own.shape[1] // 2
    distances, shards = [0], [own]
    ahead = behind = own
    for d in range(1, half):
        ahead, behind = between(d, ring.hop(ahead, True), ring.hop(behind, False))
        distances += [size - d, d]
        shards += [ahead, behind]
    halves = between(half, ring.hop(ahead[:, :middle], True), ring.hop(behind[:, middle:], False))
    return distances + [half], shards, halves


def ring_reduce(ring, grads, terms, weight, place, between):
    half, size = ring.size // 2, ring.size
    step = functools.partial(ring_step, table=ring.at, grads=grads, terms=terms, weight=weight)
    ahead, behind = step(far_kernel, distances=[half])
    for d in range(half, 0, -1):
        ahead, behind = between(half - d, ahead, ring.hop(ahead, True), ring.hop(behind, False))
        if d > 1:
            ahead, behind = step(pair_kernel, distances=[d - 1, size + 1 - d], arrived=[ahead, behind])
    return step(own_kernel, distances=[0], arrived=[ahead, behind], place=place)[0]


def shards(
    block_input, norm_gain, in_weight, conv_weight, conv_bias, select_weight, delta_weight, delta_bias,
    decay_log, skip_weight, out_weight, out_cotangent, seq_lengths, deal_order,
):
    rows_dev, width = block_input.shape
    dp_size = lax.axis_size("dp")
    tensor_size = lax.axis_size("tensor")
    pair = rows_dev // dp_size
    group_tokens = rows_dev * tensor_size
    ring = Ring("tensor")
    here = jnp.zeros((1,), jnp.int32)
    me = jnp.stack([lax.axis_index("dp"), jnp.int32(group_tokens)]).astype(jnp.int32)
    head = share(jnp.concatenate([deal_order.astype(F32), norm_gain.astype(F32)]), "dp")
    gain_values = in_order(head[:, rows_dev:], "dp").reshape(1, -1)
    send_rows, send_cot, pick, place = deal(block_input, out_cotangent, head[:, :rows_dev], gain_values, me)
    in_cat = jnp.swapaxes(after(in_weight, send_rows), 0, 1).reshape(in_weight.shape[1], -1)
    recv_rows = exchange(send_rows.reshape(dp_size, pair, -1), "dp")
    recv_rows, in_cat = lax.optimization_barrier((recv_rows, in_cat))
    in_full = lax.all_gather(in_cat, "dp", axis=0, tiled=True)
    normed = round_dot(place, recv_rows.reshape(rows_dev, -1), TN)
    channels = in_full.shape[1] // 2
    taps = conv_weight.shape[0]
    lane_width = conv_bias.shape[1] * dp_size
    own_states = decay_log.shape[1]
    states, low_rank = own_states * dp_size, delta_weight.shape[0] * dp_size
    lengths_row = seq_lengths[0]
    seq_ends = jnp.cumsum(lengths_row)
    begins = seq_ends - lengths_row
    positions = jnp.arange(group_tokens, dtype=jnp.int32)
    inside = (positions[:, None] >= begins[None, :]) & (positions[:, None] < seq_ends[None, :])
    offset = (positions - jnp.sum(jnp.where(inside, begins[None, :], 0), axis=1))[:, None]
    (projected,) = blank(((group_tokens, 2 * channels), BF16))
    half = tensor_size // 2
    NN = (((1,), (0,)), ((), ()))
    lanes_own = jnp.concatenate([conv_weight, jnp.stack([conv_bias, delta_bias, skip_weight])])
    bag = Bag(
        cot=send_cot, select=jnp.concatenate([select_weight, jnp.moveaxis(lanes_own, 0, 2)], axis=2),
        thin=jnp.concatenate([decay_log.T, delta_weight]), projected=projected)
    waiting = {"shards": [normed], "distances": [0]}

    def during_normed(d, ahead, behind):
        if d == 1:
            ahead, behind = bag.meet((ahead, behind), "select")
            bag["select"] = share(bag["select"], "dp")
            bag["own"] = out_weight
        elif d < half - 1:
            ahead, behind = bag.meet((ahead, behind), "own", "select", "cot")
            if d == 2:
                bag["cot"] = exchange(bag["cot"].reshape(dp_size, pair, -1), "dp")
        elif d >= half - 1:
            bag["projected"] = placed_product(
                ring.at, waiting["distances"], waiting["shards"], in_full, NN, bag["projected"])
            waiting["shards"], waiting["distances"] = [], []
            ahead, behind = bag.meet((ahead, behind), "projected", *(["cot"] if d == half else []))
        if d < half:
            waiting["distances"] += [tensor_size - d, d]
            waiting["shards"] += [ahead, behind]
        return ahead, behind

    distances, normed_shards, halves = ring_gather(ring, normed, during_normed)

    def rows_of(values, distance):
        return lax.dynamic_slice(values, (ring.at[distance] * rows_dev, 0), (rows_dev, values.shape[1]))

    projected = placed_halves(ring.at, distances[-1], *halves, in_full, bag["projected"])
    dealt_cot = round_dot(place, bag["cot"].reshape(rows_dev, -1), TN)
    select_matrix = jnp.moveaxis(in_order(bag["select"], "dp"), 0, 1).reshape(channels, -1)
    low_w, bc_w = select_matrix[:, :low_rank], select_matrix[:, low_rank:low_rank + 2 * states].T
    lanes_float = select_matrix[:, low_rank + 2 * states:].astype(F32).T
    conv_taps = lanes_float[:taps]
    conv_shift, delta_shift, skip_values = (lanes_float[taps + i:taps + i + 1] for i in range(3))
    activated, part = front(here, projected, offset, conv_taps, conv_shift, low_w, bc_w)
    out_full = lax.all_gather(bag["own"], "dp", axis=1, tiled=True)
    group_cot = lax.all_gather(after(dealt_cot, halves[0]), "tensor", axis=0, tiled=True)
    bag["thin"] = lax.all_gather(after(bag["thin"], part)[None], "dp", axis=0, tiled=True)
    bag["last"] = jnp.concatenate([after(v, part) for v in halves], axis=1)
    arrived = bag.meet(swap(part, "tensor"), "thin", "last")
    normed_shards = normed_shards + [bag["last"]]
    decay_full = bag["thin"][:, :own_states].reshape(states, channels)
    delta_full = bag["thin"][:, own_states:].reshape(low_rank, channels)
    decay_rate = -jnp.exp(decay_full.astype(F32))
    total = jnp.sum(arrived.astype(F32), axis=0).astype(BF16)
    pack_all = swap(jnp.broadcast_to(total[None], part.shape), "tensor")
    pre, y, gated, hist, unused_state = scan_forward(
        here, pack_all, activated, projected, offset, delta_full, delta_shift, decay_rate, skip_values,
        jnp.zeros((states, channels), F32), [], 0, tensor_size)
    gg = mm(group_cot, out_full, NT)
    held = [
        jnp.zeros((states, channels), F32),
        jnp.zeros((states, channels), F32),
        jnp.zeros((low_rank, channels), F32),
        jnp.zeros((8, channels), F32),
    ]
    mixed = lax.psum_scatter(round_dot(gated, out_full), "tensor", scatter_dimension=0, tiled=True)
    grad_projected, grad_act, grad_part, unused_carry, rate_grad, delta_weight_grad, row_grads = scan_backward(
        here, pack_all, pre, activated, projected, gg, y, offset, hist, delta_full, decay_rate, skip_values,
        held, [], tensor_size - 1, tensor_size)
    decay_grad = rate_grad * decay_rate
    def by_lane(values):
        lanes = values.reshape(-1, channels // lane_width, dp_size, lane_width // dp_size)
        return jnp.moveaxis(lanes, 2, 0).reshape(dp_size, -1)

    def pack_small(taps_sum, low_sum, bc_sum, row_grads, decay_grad, delta_weight_grad):
        select_grad = jnp.concatenate([low_sum, bc_sum.T], axis=1)
        parts = [
            by_lane(jnp.concatenate([taps_sum[:taps + 1], row_grads[:2]])),
            decay_grad.reshape(dp_size, -1),
            delta_weight_grad.reshape(dp_size, -1),
            jnp.moveaxis(select_grad.reshape(channels // lane_width, dp_size, -1), 1, 0).reshape(dp_size, -1),
        ]
        flat = jnp.concatenate(parts, axis=1)
        fill = -flat.shape[1] % 2048
        flat = jnp.pad(flat, ((0, 0), (0, fill))).astype(BF16).reshape(dp_size, -1, LANES)
        return flat, [part.shape[1] for part in parts]

    merged = channels == width // dp_size
    bag["out"] = weight_grad(
        ring.at, None, [group_cot], after(gated, grad_part), 0, channels, dp_size, True, 2 if merged else 1)
    arrived = bag.meet(swap(grad_part, "tensor"), "out")
    grad_total = jnp.sum(arrived.astype(F32), axis=0).astype(BF16)
    bag["gate"] = weight_grad(
        ring.at, distances, normed_shards, after(grad_projected, grad_total), 1, channels, dp_size, False,
        *((2, 1, [bag["out"]]) if merged else ()))
    bag["terms"] = round_dot(after(grad_projected, grad_total)[:, channels:], in_full[:, channels:], NT)
    grad_pack = bag.meet(swap(jnp.broadcast_to(grad_total[None], grad_part.shape), "tensor"), "gate", "terms")
    gate_terms = bag["terms"]
    bag["gate"] = lax.psum_scatter(bag["gate"], "dp", scatter_dimension=0, tiled=True)
    if not merged:
        bag["out"] = lax.psum_scatter(bag["out"], "dp", scatter_dimension=0, tiled=True)
    grad_projected, *sums = end(
        here, grad_pack, grad_act, activated, projected, offset, conv_taps, conv_shift, low_w, bc_w, grad_projected)
    bag["sums"] = [*sums, row_grads, decay_grad, delta_weight_grad]
    bag["mixed"] = mixed

    def during_grad(k, sent, ahead, behind):
        names = []
        if k == 0:
            bag["grads"] = grad_projected
            names = ["mixed", "sums", "grads"]
        if k == 1:
            bag["inner"] = weight_grad(ring.at, distances, normed_shards, bag["grads"], 0, channels, dp_size, False)
            bag["mixed"] = round_dot(place, bag["mixed"])
            names = ["mixed", "sums", "inner"]
        if k == half - 2:
            names = ["mixed", "flat", "gate"] + ([] if merged else ["out"])
        if k == half - 1:
            gate_grad = bag["gate"][:, channels:] if merged else bag["gate"]
            bag["in"] = jnp.concatenate([bag["inner"], gate_grad]).astype(F32)
            bag["gain"] = cube_sum(jnp.sum(in_weight.astype(F32) * bag["in"], axis=(0, 2)), "tensor", 1, 2)
            names = ["gain", "in"]
        ahead, behind = bag.meet((ahead, behind), *names)
        if k == 1:
            bag["inner"] = lax.psum_scatter(bag["inner"], "dp", scatter_dimension=0, tiled=True)
            bag["mixed"] = exchange(bag["mixed"].reshape(dp_size, pair, -1), "dp")
            flat, waiting["sizes"] = pack_small(*bag["sums"])
            bag["flat"] = swap(flat, "dp")
        return ahead, behind

    send_grad = ring_reduce(ring, grad_projected, gate_terms, in_full, place, during_grad)
    home_grad = exchange(send_grad.reshape(dp_size, pair, -1), "dp").reshape(rows_dev, -1)
    home_out = bag["mixed"].reshape(rows_dev, -1)
    out_grad = (bag["gate"][0, :channels] if merged else bag["out"][0]).astype(F32)
    in_weight_grad = bag["in"]
    gain_grad = cube_sum(after(bag["gain"], send_grad), "tensor", 2, tensor_size) / norm_gain.astype(F32)
    flat = jnp.sum(bag["flat"].astype(F32), axis=0).reshape(-1)
    small, start = [], 0
    for size in waiting["sizes"]:
        small.append(flat[start:start + size])
        start += size
    lane_grads = small[0].reshape((taps + 3,) + conv_bias.shape)
    rows_float = block_input.astype(F32)
    block_output = (rows_float + mm(pick, home_out, TN)).astype(BF16)
    inverse_rms = lax.rsqrt(jnp.mean(rows_float * rows_float, axis=1, keepdims=True) + EPSILON)
    unit_rows = rows_float * inverse_rms
    scaled = mm(pick, home_grad, TN) * gain_values
    input_grad = (
        out_cotangent.astype(F32)
        + inverse_rms * (scaled - unit_rows * jnp.mean(scaled * unit_rows, axis=1, keepdims=True))
    ).astype(BF16)
    return (
        block_output,
        input_grad,
        gain_grad,
        in_weight_grad,
        lane_grads[:taps],
        lane_grads[taps],
        small[3].reshape(select_weight.shape),
        small[2].reshape(delta_weight.shape),
        lane_grads[taps + 2],
        small[1].reshape(decay_log.shape[1], decay_log.shape[0]).T,
        lane_grads[taps + 1],
        out_grad,
    )


def solution(mesh):
    return jax.shard_map(
        shards,
        mesh=mesh,
        in_specs=(
            P(("dp", "tensor"), None),
            P("dp"),
            P(None, "dp", "tensor"),
            P(None, "tensor", "dp"),
            P("tensor", "dp"),
            P("tensor", "dp", None),
            P("dp", "tensor"),
            P("tensor", "dp"),
            P("tensor", "dp"),
            P("tensor", "dp"),
            P("tensor", "dp"),
            P(("dp", "tensor"), None),
            P("dp", None),
            P(("dp", "tensor")),
        ),
        out_specs=(
            P(("dp", "tensor"), None),
            P(("dp", "tensor"), None),
            P("dp"),
            P(None, "dp", "tensor"),
            P(None, "tensor", "dp"),
            P("tensor", "dp"),
            P("tensor", "dp", None),
            P("dp", "tensor"),
            P("tensor", "dp"),
            P("tensor", "dp"),
            P("tensor", "dp"),
            P("tensor", "dp"),
        ),
        check_vma=False,
    )
```

profile of v0, /device:TPU:0, one launch (start us, length us, event | category | flops | bytes accessed | tf_op | source)
XLA Modules:
  0.0 481.7 jit_solution(3290665542714405764)
XLA Ops:
  34.3 17.3 %collective-permute-done.7.refs_2_ = bf16[192,2048]{1,0:T(8,128)(2,1)S(1)} collective-permute-done((bf16[192,2048]{1,0:T(8,128)(2,1)S(1)}, bf16[192,2048]{1,0:T(8,128)(2,1)S(1)}, u32[]{:S(2)}, u32[]{:S(2)}) %collective-permute-start.7) | collective-permute-done | bytes 786464 | tf_op jit(solution)/shard_map/ppermute | solution.py:779
  63.9 7.7 %collective-permute-done.8.refs_3_ = bf16[192,2048]{1,0:T(8,128)(2,1)S(1)} collective-permute-done((bf16[192,2048]{1,0:T(8,128)(2,1)}, bf16[192,2048]{1,0:T(8,128)(2,1)S(1)}, u32[]{:S(2)}, u32[]{:S(2)}) %collective-permute-start.8) | collective-permute-done | bytes 786464 | tf_op jit(solution)/shard_map/ppermute | solution.py:779
  78.2 12.0 %placed_product.2.refs_3_ = bf16[1536,1024]{1,0:T(8,128)(2,1)} custom-call(s32[8]{0:T(128)S(1)} %dynamic-slice_bitcast_fusion.table_ref, bf16[192,2048]{1,0:T(8,128)(2,1)} %copy-done.4, bf16[192,2048]{1,0:T(8,128)(2,1)} %collective-permute-done.6.refs_1_, bf16[192,2048]{1,0:T(8,128)(2,1)} %copy-done.6, ...), custom_call_target="tpu_custom_call", output_to_operand_aliasing={{}: (7, {})} | custom-call | flops 1 | bytes 1 | tf_op jit(solution)/shard_map/placed_product/pallas_call | solution.py:521
  94.9 6.9 %placed_product.3.refs_8_ = bf16[1536,1024]{1,0:T(8,128)(2,1)} custom-call(s32[8]{0:T(128)S(1)} %dynamic-slice_bitcast_fusion.table_ref, bf16[192,2048]{1,0:T(8,128)(2,1)} %copy-done.5, bf16[192,2048]{1,0:T(8,128)(2,1)} %collective-permute-done.14.refs_1_.refs_6_, ...), custom_call_target="tpu_custom_call", output_to_operand_aliasing={{}: (4, {})} | custom-call | flops 1 | bytes 1 | tf_op jit(solution)/shard_map/placed_product/pallas_call | solution.py:521
  110.9 7.8 %front.1 = (bf16[1536,512]{1,0:T(8,128)(2,1)}, bf16[8,240,128]{2,1,0:T(8,128)(2,1)}) custom-call(s32[1]{0:T(128)} %constant.79.clone.1.me_ref, bf16[1536,1024]{1,0:T(8,128)(2,1)} %placed_halves.1.inner_ref.gate_ref.prior_ref, s32[1536,1]{1,0:T(8,128)S(1)} %reshape_subtract_fusion.offset_ref, f32[4,512]{1,0:T(4,128)S(1)} %slice.255.taps_ref, ...), custom_call_target="tpu_custom_call" | custom-call | flops 1 | bytes 1 | tf_op jit(solution)/shard_map/front/pallas_call | solution.py:87
  123.6 5.5 %all-gather.1 = bf16[4,36,512]{2,1,0:T(8,128)(2,1)S(1)} all-gather(bf16[1,36,512]{2,1,0:T(8,128)(2,1)S(1)} %bitcast.151), channel_id=2, replica_groups=mesh['dp'=4,'tensor'=8] {'dp'}, dimensions={0}, use_global_device_ids=true | all-gather | bytes 184320 | tf_op jit(solution)/shard_map/all_gather | solution.py:880
  131.0 19.8 %all-to-all-done = bf16[8,240,128]{2,1,0:T(8,128)(2,1)S(1)} async-done(((bf16[8,240,128]{2,1,0:T(8,128)(2,1)}), bf16[8,240,128]{2,1,0:T(8,128)(2,1)S(1)}, u32[]{:S(2)}, u32[]{:S(2)}) %all-to-all-start) | async-done | bytes 491552 | tf_op jit(solution)/shard_map/all_to_all | solution.py:725
  155.6 25.0 %all-to-all-done.1.pack_ref = bf16[8,240,128]{2,1,0:T(8,128)(2,1)S(1)} async-done(((bf16[8,240,128]{2,1,0:T(8,128)(2,1)}), bf16[8,240,128]{2,1,0:T(8,128)(2,1)S(1)}, u32[]{:S(2)}, u32[]{:S(2)}) %all-to-all-start.1) | async-done | bytes 491552 | tf_op jit(solution)/shard_map/all_to_all | solution.py:725
  180.6 26.0 %scan_forward.1 = (f32[1536,512]{1,0:T(8,128)}, f32[1536,512]{1,0:T(8,128)}, bf16[1536,512]{1,0:T(8,128)(2,1)}, bf16[24576,512]{1,0:T(8,128)(2,1)}, f32[16,512]{1,0:T(8,128)}) custom-call(s32[1]{0:T(128)} %constant.79.clone.1.me_ref, bf16[8,240,128]{2,1,0:T(8,128)(2,1)S(1)} %all-to-all-done.1.pack_ref, bf16[1536,512]{1,0:T(8,128)(2,1)} %get-tuple-element.127.act_ref, ...), custom_call_target="tpu_custom_call" | custom-call | flops 1 | bytes 1 | tf_op jit(solution)/shard_map/scan_forward/pallas_call | solution.py:183
  206.6 8.2 %convolution_convert_fusion = bf16[1536,2048]{1,0:T(8,128)(2,1)} fusion(bf16[1536,512]{1,0:T(8,128)(2,1)} %get-tuple-element.137.refs_1_, bf16[512,2048]{1,0:T(8,128)(2,1)} %all-gather.10.cloned.1.call-done), kind=kOutput, calls=%fused_computation | convolution fusion | flops 3224371200 | bytes 9961472 | tf_op jit(solution)/shard_map/dot_general | solution.py:31
  218.1 8.5 %fusion.27.gg_ref = f32[1536,512]{1,0:T(8,128)} fusion(bf16[1536,2048]{1,0:T(8,128)(2,1)} %all-gather.8.cloned.1.call-done.refs_0_, bf16[512,2048]{1,0:T(8,128)(2,1)} %all-gather.10.cloned.1.call-done), kind=kOutput, calls=%fused_computation.95 | convolution fusion | flops 3221225472 | bytes 11534336 | tf_op jit(solution)/shard_map/dot_general | solution.py:31
  226.7 62.9 %scan_backward.1 = (bf16[1536,1024]{1,0:T(8,128)(2,1)}, f32[1536,512]{1,0:T(8,128)}, bf16[8,240,128]{2,1,0:T(8,128)(2,1)}, f32[16,512]{1,0:T(8,128)}, f32[16,512...) custom-call(s32[1]{0:T(128)} %constant.79.clone.1.me_ref, ...), custom_call_target="tpu_custom_call" | custom-call | flops 1 | bytes 1 | tf_op jit(solution)/shard_map/scan_backward/pallas_call | solution.py:328
  293.3 8.4 %weight_grad.3.refs_16_ = bf16[4,1024,512]{2,1,0:T(8,128)(2,1)} custom-call(s32[8]{0:T(128)S(1)} %dynamic-slice_bitcast_fusion.table_ref, bf16[1536,2048]{1,0:T(8,128)(2,1)} %all-gather.8.cloned.1.call-done.refs_0_, bf16[1536,512]{1,0:T(8,128)(2,1)} %get-tuple-element.137.refs_1_), custom_call_target="tpu_custom_call" | custom-call | flops 1 | bytes 1 | tf_op jit(solution)/shard_map/weight_grad/pallas_call | solution.py:476
  301.7 5.9 %all-to-all-done.2 = bf16[8,240,128]{2,1,0:T(8,128)(2,1)S(1)} async-done(((bf16[8,240,128]{2,1,0:T(8,128)(2,1)}), bf16[8,240,128]{2,1,0:T(8,128)(2,1)S(1)}, u32[]{:S(2)}, u32[]{:S(2)}) %all-to-all-start.2) | async-done | bytes 491552 | tf_op jit(solution)/shard_map/all_to_all | solution.py:725
  312.2 9.0 %weight_grad.4 = bf16[4,1024,512]{2,1,0:T(8,128)(2,1)} custom-call(s32[8]{0:T(128)S(1)} %dynamic-slice_bitcast_fusion.table_ref, bf16[192,2048]{1,0:T(8,128)(2,1)} %copy-done.4, bf16[192,2048]{1,0:T(8,128)(2,1)} %collective-permute-done.6.refs_1_, bf16[192,2048]{1,0:T(8,128)(2,1)} %copy-done.6, ...), custom_call_target="tpu_custom_call", output_to_operand_aliasing={{}: (17, {})} | custom-call | flops 1 | bytes 1 | tf_op jit(solution)/shard_map/weight_grad/pallas_call | solution.py:476
  321.2 8.2 %convolution_convert_fusion.1.t_ref.ta_ref.tb_ref = bf16[1536,2048]{1,0:T(8,128)(2,1)} fusion(bf16[2048,1024]{1,0:T(8,128)(2,1)} %all-gather.6.cloned.1.call-done.refs_5_.refs_2_.refs_0_.refs_1_.refs_3_.refs_4_.refs_6_.refs_7_, bf16[1536,1024]{1,0:T(8,128)(2,1)} %get-tuple-element.141.refs_8_.refs_9_.refs_10_.refs_11_.refs_12_.refs_13_.refs_14_.refs_15_.grad_ref), kind=kOutput, calls=%fused_computation.1 | convolution fusion | flops 3224371200 | bytes 9961472 | tf_op jit(solution)/shard_map/dot_general | solution.py:31
  329.4 9.4 %all-to-all-done.3.pack_ref = bf16[8,240,128]{2,1,0:T(8,128)(2,1)S(1)} async-done(((bf16[8,240,128]{2,1,0:T(8,128)(2,1)}), bf16[8,240,128]{2,1,0:T(8,128)(2,1)S(1)}, u32[]{:S(2)}, u32[]{:S(2)}) %all-to-all-start.3) | async-done | bytes 491552 | tf_op jit(solution)/shard_map/all_to_all | solution.py:725
  338.9 11.3 %end.1 = (bf16[1536,1024]{1,0:T(8,128)(2,1)}, f32[8,512]{1,0:T(8,128)S(1)}, f32[512,128]{1,0:T(8,128)S(1)}, f32[32,512]{1,0:T(8,128)S(1)}) custom-call(s32[1]{0:T(128)} %constant.79.clone.1.me_ref, bf16[8,240,128]{2,1,0:T(8,128)(2,1)S(1)} %all-to-all-done.3.pack_ref, f32[1536,512]{1,0:T(8,128)} %get-tuple-element.144.gact_ref, ...), custom_call_target="tpu_custom_call", output_to_operand_aliasing={{0}: (11, {})} | custom-call | flops 1 | bytes 1 | tf_op jit(solution)/shard_map/end/pallas_call | solution.py:408
  356.4 6.0 %collective-permute-done.20.refs_4_ = bf16[192,1024]{1,0:T(8,128)(2,1)S(1)} collective-permute-done((bf16[192,1024]{1,0:T(8,128)(2,1)}, bf16[192,1024]{1,0:T(8,128)(2,1)S(1)}, u32[]{:S(2)}, u32[]{:S(2)}) %collective-permute-start.20) | collective-permute-done | bytes 393248 | tf_op jit(solution)/shard_map/ppermute | solution.py:779
  371.3 9.1 %weight_grad.5 = bf16[4,512,512]{2,1,0:T(8,128)(2,1)} custom-call(s32[8]{0:T(128)S(1)} %dynamic-slice_bitcast_fusion.table_ref, bf16[192,2048]{1,0:T(8,128)(2,1)} %copy-done.4, bf16[192,2048]{1,0:T(8,128)(2,1)} %collective-permute-done.6.refs_1_, bf16[192,2048]{1,0:T(8,128)(2,1)} %copy-done.6, bf16[192,2048]{1,0:T(8,128)(2,1)} %copy-done.7, ...), custom_call_target="tpu_custom_call" | custom-call | flops 1 | bytes 1 | tf_op jit(solution)/shard_map/weight_grad/pallas_call | solution.py:476
  380.9 5.5 %collective-permute-done.22.refs_4_ = bf16[192,2048]{1,0:T(8,128)(2,1)} collective-permute-done((bf16[192,2048]{1,0:T(8,128)(2,1)}, bf16[192,2048]{1,0:T(8,128)(2,1)}, u32[]{:S(2)}, u32[]{:S(2)}) %collective-permute-start.22) | collective-permute-done | bytes 786464 | tf_op jit(solution)/shard_map/ppermute | solution.py:779
  414.8 6.3 %collective-permute-done.24.refs_4_ = bf16[192,2048]{1,0:T(8,128)(2,1)} collective-permute-done((bf16[192,2048]{1,0:T(8,128)(2,1)}, bf16[192,2048]{1,0:T(8,128)(2,1)}, u32[]{:S(2)}, u32[]{:S(2)}) %collective-permute-start.24) | collective-permute-done | bytes 786464 | tf_op jit(solution)/shard_map/ppermute | solution.py:779
  438.6 9.6 %collective-permute-done.31 = f32[512]{0:T(512)S(1)} collective-permute-done((f32[512]{0:T(512)S(1)}, f32[512]{0:T(512)S(1)}, u32[]{:S(2)}, u32[]{:S(2)}) %collective-permute-start.31) | collective-permute-done | bytes 2080 | tf_op jit(solution)/shard_map/ppermute | solution.py:716
  448.2 5.8 %own_kernel.1 = bf16[192,2048]{1,0:T(8,128)(2,1)} custom-call(s32[8]{0:T(128)S(1)} %dynamic-slice_bitcast_fusion.table_ref, bf16[1536,1024]{1,0:T(8,128)(2,1)} %get-tuple-element.159.g_ref.ga_ref.gb_ref.refs_8_.refs_9_.refs_10_.refs_11_.refs_12_.refs_13_.refs_14_.refs_15_, bf16[1536,2048]{1,0:T(8,128)(2,1)} %convolution_convert_fusion.1.t_ref.ta_ref.tb_ref, ...), custom_call_target="tpu_custom_call" | custom-call | flops 1 | bytes 1 | tf_op jit(solution)/shard_map/own_kernel/pallas_call | solution.py:625
  (284 shorter events, 164.2 us)
Async XLA Ops:
  7.2 71.0 %all-gather.6.cloned.1.call-start = ((), (), s32[]{:S(2)}) async-start(), calls=%async_computation.8 | async-start | bytes 5242880 | tf_op jit(solution)/shard_map/all_gather | solution.py:824
  31.5 175.1 %all-gather.10.cloned.1.call-start = ((), (), s32[]{:S(2)}) async-start(), calls=%async_computation.10 | async-start | bytes 2621440 | tf_op jit(solution)/shard_map/all_gather | solution.py:878
  32.0 19.6 %collective-permute-start.7 = (bf16[192,2048]{1,0:T(8,128)(2,1)S(1)}, bf16[192,2048]{1,0:T(8,128)(2,1)S(1)}, u32[]{:S(2)}, u32[]{:S(2)}) collective-permute-start(bf16[192,2048]{1,0:T(8,128)(2,1)S(1)} %convolution_convert_fusion.4.refs_0_), channel_id=1, source_target_pairs={{1,0},{3,1},{5,3},{7,5},{6,7},{4,6},{2,4},{0,2},{9,8},{11,9},{13,1... | collective-permute-start | bytes 2359304 | tf_op jit(solution)/shard_map/ppermute | solution.py:779
  33.6 19.4 %collective-permute-start.6 = (bf16[192,2048]{1,0:T(8,128)(2,1)S(1)}, bf16[192,2048]{1,0:T(8,128)(2,1)}, u32[]{:S(2)}, u32[]{:S(2)}) collective-permute-start(bf16[192,2048]{1,0:T(8,128)(2,1)S(1)} %convolution_convert_fusion.4.refs_0_), channel_id=1, source_target_pairs={{0,1},{1,3},{3,5},{5,7},{7,6},{6,4},{4,2},{2,0},{8,9},{9,11},{11,1... | collective-permute-start | bytes 2359304 | tf_op jit(solution)/shard_map/ppermute | solution.py:779
  53.0 18.6 %collective-permute-start.8 = (bf16[192,2048]{1,0:T(8,128)(2,1)}, bf16[192,2048]{1,0:T(8,128)(2,1)S(1)}, u32[]{:S(2)}, u32[]{:S(2)}) collective-permute-start(bf16[192,2048]{1,0:T(8,128)(2,1)} %collective-permute-done.6.refs_1_), channel_id=1, source_target_pairs={{0,1},{1,3},{3,5},{5,7},{7,6},{6,4},{4,2},{2,0},{8,9},{9,11},{11,1... | collective-permute-start | bytes 2359304 | tf_op jit(solution)/shard_map/ppermute | solution.py:779
  53.4 18.2 %collective-permute-start.9 = (bf16[192,2048]{1,0:T(8,128)(2,1)S(1)}, bf16[192,2048]{1,0:T(8,128)(2,1)S(1)}, u32[]{:S(2)}, u32[]{:S(2)}) collective-permute-start(bf16[192,2048]{1,0:T(8,128)(2,1)S(1)} %collective-permute-done.7.refs_2_), channel_id=1, source_target_pairs={{1,0},{3,1},{5,3},{7,5},{6,7},{4,6},{2,4},{0,2},{9,8},{11,9},{13,1... | collective-permute-start | bytes 2359304 | tf_op jit(solution)/shard_map/ppermute | solution.py:779
  72.6 145.4 %all-gather.8.cloned.1.call-start = ((), (), s32[]{:S(2)}) async-start(), calls=%async_computation.9 | async-start | bytes 7077888 | tf_op jit(solution)/shard_map/all_gather | solution.py:879
  72.7 17.4 %collective-permute-start.13 = (bf16[192,2048]{1,0:T(8,128)(2,1)S(1)}, bf16[192,2048]{1,0:T(8,128)(2,1)S(1)}, u32[]{:S(2)}, u32[]{:S(2)}) collective-permute-start(bf16[192,2048]{1,0:T(8,128)(2,1)S(1)} %collective-permute-done.8.refs_3_), channel_id=1, source_target_pairs={{0,1},{1,3},{3,5},{5,7},{7,6},{6,4},{4,2},{2,0},{8,9},{9,11},{11,1... | collective-permute-start | bytes 2359304 | tf_op jit(solution)/shard_map/ppermute | solution.py:779
  75.6 19.1 %collective-permute-start.19 = (bf16[48,2048]{1,0:T(8,128)(2,1)}, bf16[48,2048]{1,0:T(8,128)(2,1)S(1)}, u32[]{:S(2)}, u32[]{:S(2)}) collective-permute-start(bf16[48,2048]{1,0:T(8,128)(2,1)} %get-tuple-element.206), channel_id=1, source_target_pairs={{0,24},{8,16},{16,8},{24,0},{1,25},{9,17},{17,9},{25,1},{2,26},{10... | collective-permute-start | bytes 589832 | tf_op jit(solution)/shard_map/ppermute | solution.py:716
  75.6 19.1 %collective-permute-start.18 = (bf16[48,2048]{1,0:T(8,128)(2,1)}, bf16[48,2048]{1,0:T(8,128)(2,1)S(1)}, u32[]{:S(2)}, u32[]{:S(2)}) collective-permute-start(bf16[48,2048]{1,0:T(8,128)(2,1)} %get-tuple-element.207), channel_id=1, source_target_pairs={{0,16},{8,24},{16,0},{24,8},{1,17},{9,25},{17,1},{25,9},{2,18},{10... | collective-permute-start | bytes 589832 | tf_op jit(solution)/shard_map/ppermute | solution.py:716
  76.7 18.0 %collective-permute-start.17 = (bf16[48,2048]{1,0:T(8,128)(2,1)}, bf16[48,2048]{1,0:T(8,128)(2,1)S(1)}, u32[]{:S(2)}, u32[]{:S(2)}) collective-permute-start(bf16[48,2048]{1,0:T(8,128)(2,1)} %get-tuple-element.208), channel_id=1, source_target_pairs={{0,8},{8,0},{16,24},{24,16},{1,9},{9,1},{17,25},{25,17},{2,10},{10... | collective-permute-start | bytes 589832 | tf_op jit(solution)/shard_map/ppermute | solution.py:716
  118.7 32.1 %all-to-all-start = ((bf16[8,240,128]{2,1,0:T(8,128)(2,1)}), bf16[8,240,128]{2,1,0:T(8,128)(2,1)S(1)}, u32[]{:S(2)}, u32[]{:S(2)}) async-start(bf16[8,240,128]{2,1,0:T(8,128)(2,1)} %get-tuple-element.122), calls=%async_computation | async-start | bytes 983040 | tf_op jit(solution)/shard_map/all_to_all | solution.py:725
  151.8 28.8 %all-to-all-start.1 = ((bf16[8,240,128]{2,1,0:T(8,128)(2,1)}), bf16[8,240,128]{2,1,0:T(8,128)(2,1)S(1)}, u32[]{:S(2)}, u32[]{:S(2)}) async-start(bf16[8,240,128]{2,1,0:T(8,128)(2,1)} %broadcast_in_dim.22), calls=%async_computation.1 | async-start | bytes 983040 | tf_op jit(solution)/shard_map/all_to_all | solution.py:725
  155.3 208.4 %reduce-scatter.4.cloned.1.call-start = ((), (), s32[]{:S(2)}) async-start(), calls=%async_computation.11 | async-start | bytes 7077888 | tf_op jit(solution)/shard_map/reduce_scatter | solution.py:899
  289.6 18.0 %all-to-all-start.2 = ((bf16[8,240,128]{2,1,0:T(8,128)(2,1)}), bf16[8,240,128]{2,1,0:T(8,128)(2,1)S(1)}, u32[]{:S(2)}, u32[]{:S(2)}) async-start(bf16[8,240,128]{2,1,0:T(8,128)(2,1)} %get-tuple-element.135), calls=%async_computation.2 | async-start | bytes 983040 | tf_op jit(solution)/shard_map/all_to_all | solution.py:725
  308.5 30.3 %all-to-all-start.3 = ((bf16[8,240,128]{2,1,0:T(8,128)(2,1)}), bf16[8,240,128]{2,1,0:T(8,128)(2,1)S(1)}, u32[]{:S(2)}, u32[]{:S(2)}) async-start(bf16[8,240,128]{2,1,0:T(8,128)(2,1)} %broadcast_in_dim.25), calls=%async_computation.3 | async-start | bytes 983040 | tf_op jit(solution)/shard_map/all_to_all | solution.py:725
  312.2 110.6 %reduce-scatter.6.cloned.1.call-start = ((), (), s32[]{:S(2)}) async-start(), calls=%async_computation.12 | async-start | bytes 5242880 | tf_op jit(solution)/shard_map/reduce_scatter | solution.py:932
  338.9 94.0 %reduce-scatter.8.cloned.1.call-start = ((), (), s32[]{:S(2)}) async-start(), calls=%async_computation.13 | async-start | bytes 2621440 | tf_op jit(solution)/shard_map/reduce_scatter | solution.py:958
  370.9 19.1 %collective-permute-start.23 = (bf16[192,2048]{1,0:T(8,128)(2,1)}, bf16[192,2048]{1,0:T(8,128)(2,1)}, u32[]{:S(2)}, u32[]{:S(2)}) collective-permute-start(bf16[192,2048]{1,0:T(8,128)(2,1)} %get-tuple-element.158), channel_id=1, source_target_pairs={{1,0},{3,1},{5,3},{7,5},{6,7},{4,6},{2,4},{0,2},{9,8},{11,9},{13,1... | collective-permute-start | bytes 2359304 | tf_op jit(solution)/shard_map/ppermute | solution.py:779
  392.4 22.4 %all-to-all-start.4 = ((bf16[4,320,128]{2,1,0:T(8,128)(2,1)}), bf16[4,320,128]{2,1,0:T(8,128)(2,1)S(1)}, u32[]{:S(2)}, u32[]{:S(2)}) async-start(bf16[4,320,128]{2,1,0:T(8,128)(2,1)} %bitcast.119), calls=%async_computation.5 | async-start | bytes 655360 | tf_op jit(solution)/shard_map/all_to_all | solution.py:725
  400.8 20.3 %collective-permute-start.24 = (bf16[192,2048]{1,0:T(8,128)(2,1)}, bf16[192,2048]{1,0:T(8,128)(2,1)}, u32[]{:S(2)}, u32[]{:S(2)}) collective-permute-start(bf16[192,2048]{1,0:T(8,128)(2,1)} %get-tuple-element.169), channel_id=1, source_target_pairs={{0,1},{1,3},{3,5},{5,7},{7,6},{6,4},{4,2},{2,0},{8,9},{9,11},{11,1... | collective-permute-start | bytes 2359304 | tf_op jit(solution)/shard_map/ppermute | solution.py:779
  402.6 20.2 %collective-permute-start.25 = (bf16[192,2048]{1,0:T(8,128)(2,1)}, bf16[192,2048]{1,0:T(8,128)(2,1)}, u32[]{:S(2)}, u32[]{:S(2)}) collective-permute-start(bf16[192,2048]{1,0:T(8,128)(2,1)} %get-tuple-element.170), channel_id=1, source_target_pairs={{1,0},{3,1},{5,3},{7,5},{6,7},{4,6},{2,4},{0,2},{9,8},{11,9},{13,1... | collective-permute-start | bytes 2359304 | tf_op jit(solution)/shard_map/ppermute | solution.py:779
  427.8 20.4 %collective-permute-start.29 = (bf16[192,2048]{1,0:T(8,128)(2,1)}, bf16[192,2048]{1,0:T(8,128)(2,1)}, u32[]{:S(2)}, u32[]{:S(2)}) collective-permute-start(bf16[192,2048]{1,0:T(8,128)(2,1)} %get-tuple-element.182), channel_id=1, source_target_pairs={{0,1},{1,3},{3,5},{5,7},{7,6},{6,4},{4,2},{2,0},{8,9},{9,11},{11,1... | collective-permute-start | bytes 2359304 | tf_op jit(solution)/shard_map/ppermute | solution.py:779
  429.3 18.9 %collective-permute-start.30 = (bf16[192,2048]{1,0:T(8,128)(2,1)}, bf16[192,2048]{1,0:T(8,128)(2,1)}, u32[]{:S(2)}, u32[]{:S(2)}) collective-permute-start(bf16[192,2048]{1,0:T(8,128)(2,1)} %get-tuple-element.183), channel_id=1, source_target_pairs={{1,0},{3,1},{5,3},{7,5},{6,7},{4,6},{2,4},{0,2},{9,8},{11,9},{13,1... | collective-permute-start | bytes 2359304 | tf_op jit(solution)/shard_map/ppermute | solution.py:779
  (58 other events, 456.4 us)
Sparse Core Ops, SparseCore 0:
  31.6 38.1 all-gather.5
  72.8 26.8 all-gather.9
  105.1 112.9 all-gather.7
  221.5 131.0 reduce-scatter.3
  355.0 43.1 reduce-scatter.5
  401.4 31.4 reduce-scatter.7
where the time goes:
time: 490 us; the launch traced here: 482 us
  Pallas kernels  185 us (38%)
  waiting for transfers between devices  164 us (33%)
  starting transfers between devices  51.4 us (10%)
  matrix products  28.8 us (6%)
  local copies, waits for them, and re-layouts  18.3 us (4%)
  between operations  15.4 us (3%)
  other arithmetic  13.7 us (3%)
  blocking collectives  5.52 us (1%)
    pallas_call x1, Pallas kernels, scan_backward(): pl.pallas_call(functools.partial(backward_kernel, len(whole)), name='scan...  62.9 us
    all_to_all x5, waiting for transfers between devices, swap(): return lax.all_to_all(values, axis, split_axis=0, concat_axis=0, tiled=True)  60.2 us
    ppermute x16, waiting for transfers between devices, hop(): lax.ppermute(value, self.axis, self.forward if ahead else self.backward)  54.4 us
    ppermute x21, waiting for transfers between devices, flip(): lax.ppermute(value, axis, [(i, i ^ bit) for i in range(lax.axis_size(axis...  44.3 us
    dot_general x8, matrix products, mm(): return lax.dot_general(a, b, dims, preferred_element_type=F32)  28.8 us
    pallas_call x3, Pallas kernels, weight_grad(): pl.pallas_call(functools.partial(weight_grad_kernel, count, turned), name...  26.5 us
    pallas_call x1, Pallas kernels, scan_forward(): pl.pallas_call(functools.partial(forward_kernel, len(whole)), name='scan_...  26 us
    pallas_call x5, Pallas kernels, ring_step(): pl.pallas_call(functools.partial(kernel, cuts, halves=True) if small else...  24.7 us
  transfers between devices with their start and end apart: 48, of which 31 were waited for; matrix products, arithmetic and copies ran while one was open for 11% of the time, Pallas kernels for 37%

commit v1 on v0

--- a/solution.py
+++ b/solution.py
@@ -131,7 +131,7 @@
 
 
 def forward_kernel(kept, me_ref, pack_ref, act_ref, gate_ref, offset_ref, dw_ref, bias_ref, rate_ref, skip_ref, h_in, *rest):
-    pre_ref, y_ref, gated_ref, hist_ref, h_s, dtm_s, u_s = rest[kept:]
+    dt_ref, sp_ref, y_ref, gated_ref, hist_ref, h_s, dtm_s, u_s = rest[kept:]
     states, channels = rate_ref.shape
     chunk = act_ref.shape[0]
 
@@ -142,8 +142,10 @@
     low, bt, ct = read_packed(pack_ref, states)
     wide = bt.shape[1]
     pre = mm(low, dw_ref[...]) + bias_ref[...]
-    pre_ref[...] = pre
-    dt = softplus(pre)
+    small = jnp.exp(-jnp.abs(pre))
+    dt = jnp.maximum(pre, 0.0) + jnp.log1p(small)
+    dt_ref[...] = dt
+    sp_ref[...] = jnp.where(pre >= 0.0, 1.0, small) / (1.0 + small)
     act = act_ref[...].astype(F32)
     u_s[...] = dt * act
     dtm_s[...] = jnp.where(offset_ref[...] == 0, FAR, dt)
@@ -201,6 +203,7 @@
                 pl.BlockSpec((chunk, channels), row),
                 pl.BlockSpec((chunk, channels), row),
                 pl.BlockSpec((chunk, channels), row),
+                pl.BlockSpec((chunk, channels), row),
                 pl.BlockSpec((chunk * states, channels), row),
                 pl.BlockSpec(rate.shape, fixed),
             ],
@@ -212,6 +215,7 @@
         out_shape=[
             pltpu.HBM((tokens, channels), F32),
             pltpu.HBM((tokens, channels), F32),
+            pltpu.HBM((tokens, channels), F32),
             pltpu.HBM((tokens, channels), BF16),
             pltpu.HBM((tokens * states, channels), BF16),
             jax.ShapeDtypeStruct(rate.shape, F32),
@@ -222,10 +226,10 @@
     )(me, pack, in_hbm(act), in_hbm(projected), offset, delta_w, bias, rate, skip, held, *(in_hbm(v) for v in whole))
 
 
-def backward_kernel(kept, me_ref, pack_ref, pre_ref, act_ref, gate_ref, gg_ref, y_ref, offset_ref,
+def backward_kernel(kept, me_ref, pack_ref, dt_ref, sp_ref, act_ref, gate_ref, gg_ref, y_ref, offset_ref,
                     hist_ref, prior_ref, dw_ref, rate_ref, skip_ref, carry_in, rgrad_in, dwgrad_in, rows_in, *rest):
     (ggate_ref, gact_ref, part_ref, carry_s, rgrad_ref, dwgrad_ref, rows_ref,
-     dtm_s, u_s, dt_s, gy_s, drive_s, decay_s, wide_s, adj_s, thr_s) = rest[kept:]
+     dtm_s, u_s, gy_s, drive_s, decay_s, wide_s, adj_s, thr_s) = rest[kept:]
     states, channels = rate_ref.shape
     chunk = act_ref.shape[0]
 
@@ -238,10 +242,8 @@
 
     low, bt, ct = read_packed(pack_ref, states)
     wide = bt.shape[1]
-    pre = pre_ref[...]
-    dt = softplus(pre)
+    dt = dt_ref[...]
     act = act_ref[...].astype(F32)
-    dt_s[...] = dt
     u_s[...] = dt * act
     dtm_s[...] = jnp.where(offset_ref[...] == 0, FAR, dt)
     gate = gate_ref[...].astype(F32)
@@ -259,7 +261,7 @@
         base = pl.multiple_of(g * STEP, STEP)
         cg = pltpu.roll(ct, wide - base, 1)
         dtm = dtm_s[pl.ds(base, STEP), :]
-        dts = dt_s[pl.ds(base, STEP), :]
+        dts = dt_ref[pl.ds(base, STEP), :]
         gys = gy_s[pl.ds(base, STEP), :]
         for j in reversed(range(STEP)):
             if j > 0:
@@ -302,14 +304,14 @@
     wide_s[states:2 * states, 0:chunk] = mm(tiles, gc_all.astype(BF16))
     drive = drive_s[...]
     gact_ref[...] = drive * dt + gy * skip_ref[...]
-    gpre = ((drive * act + decay_s[...]) * sigmoid(pre)).astype(BF16)
+    gpre = ((drive * act + decay_s[...]) * sp_ref[...]).astype(BF16)
     rows_ref[0:1, :] += jnp.sum(gy * act, axis=0, keepdims=True)
     rows_ref[1:2, :] += jnp.sum(gpre.astype(F32), axis=0, keepdims=True)
     dwgrad_ref[...] += mm(low, gpre, TN)
     write_packed(part_ref, mm(gpre, dw_ref[...], NT), wide_s)
 
 
-def scan_backward(me, pack, pre, act, projected, gg, y, offset, hist, delta_w, rate, skip, held, whole, last, steps):
+def scan_backward(me, pack, dt, sp, act, projected, gg, y, offset, hist, delta_w, rate, skip, held, whole, last, steps):
     tokens, channels = act.shape
     states = rate.shape[0]
     chunk = ROWS[0]
@@ -335,6 +337,7 @@
                 pl.BlockSpec((1,) + pack.shape[1:], run),
                 pl.BlockSpec((chunk, channels), row),
                 pl.BlockSpec((chunk, channels), row),
+                pl.BlockSpec((chunk, channels), row),
                 pl.BlockSpec((chunk, channels), second),
                 pl.BlockSpec((chunk, channels), row),
                 pl.BlockSpec((chunk, channels), row),
@@ -346,15 +349,15 @@
                 pl.BlockSpec(skip.shape, fixed),
             ] + sums + [pl.BlockSpec(memory_space=pl.ANY)] * len(whole),
             out_specs=blocks + sums,
-            scratch_shapes=[pltpu.VMEM((chunk, channels), F32)] * 6
+            scratch_shapes=[pltpu.VMEM((chunk, channels), F32)] * 5
             + [pltpu.VMEM((2 * states, 2 * LANES), F32)]
             + [pltpu.VMEM((chunk * states, channels), BF16)] * 2,
         ),
         out_shape=shapes + [jax.ShapeDtypeStruct(v.shape, F32) for v in held],
-        input_output_aliases={17 + i: i for i in range(len(whole))},
+        input_output_aliases={18 + i: i for i in range(len(whole))},
         compiler_params=pltpu.CompilerParams(dimension_semantics=("arbitrary",), vmem_limit_bytes=24 << 20),
         cost_estimate=SMALL,
-    )(me, pack, in_hbm(pre), in_hbm(act), in_hbm(projected), in_hbm(gg), in_hbm(y), offset, in_hbm(hist), in_hbm(hist), delta_w, rate, skip, *held, *(in_hbm(v) if k == 1 else v for k, v in enumerate(whole)))
+    )(me, pack, in_hbm(dt), in_hbm(sp), in_hbm(act), in_hbm(projected), in_hbm(gg), in_hbm(y), offset, in_hbm(hist), in_hbm(hist), delta_w, rate, skip, *held, *(in_hbm(v) if k == 1 else v for k, v in enumerate(whole)))
 
 
 def end_kernel(me_ref, pack_ref, gact_ref, act_ref, inner_ref, prior_ref, offset_ref, taps_ref, shift_ref, low_ref, bc_ref, grad_ref,
@@ -600,16 +603,18 @@
 
 
 def own_kernel(cuts, table_ref, g_ref, t_ref, *refs):
-    w_refs, (ra_ref, rb_ref, place_ref, out_ref) = refs[:cuts], refs[cuts:]
+    w_refs, (ra_ref, rb_ref, place_ref), outs = refs[:cuts], refs[cuts:cuts + 3], refs[cuts + 3:]
     columns = w_refs[0].shape[0]
+    pair = outs[0].shape[0]
     for c in range(cuts):
         at = slice(c * columns, (c + 1) * columns)
         total = mm(g_ref[...], w_refs[c][...], NT) + t_ref[:, at].astype(F32)
-        total = total + ra_ref[:, at].astype(F32) + rb_ref[:, at].astype(F32)
-        out_ref[:, at] = mm(place_ref[...], total.astype(BF16)).astype(BF16)
-
-
-def ring_step(kernel, table, distances, grads, terms, weight, arrived=(), place=None):
+        total = (total + ra_ref[:, at].astype(F32) + rb_ref[:, at].astype(F32)).astype(BF16)
+        for d, out_ref in enumerate(outs):
+            out_ref[:, at] = mm(place_ref[d * pair:(d + 1) * pair, :], total).astype(BF16)
+
+
+def ring_step(kernel, table, distances, grads, terms, weight, arrived=(), place=None, pieces=1):
     rows, cuts = ROWS[0], 4
     width, channels = weight.shape[0], weight.shape[1] // 2
     half, columns = width // 2, width // (2 * cuts)
@@ -619,7 +624,7 @@
     if far:
         outs, shape = [fixed, fixed], (rows, half)
     else:
-        outs, shape = [side, side] if place is None else [side], (rows, width)
+        outs, shape = [side, side] if place is None else [side] * pieces, (rows // pieces, width)
     small = not far and arrived[0].shape[1] == half
     extra = [] if place is None else [place]
     return pl.pallas_call(
@@ -633,7 +638,7 @@
             + [pl.BlockSpec((columns, channels), lambda i, table, c=c: (i * cuts + c, 0)) for c in range(cuts)]
             + [pl.BlockSpec((rows, half), fixed if small else side) for v in arrived]
             + [pl.BlockSpec(v.shape, fixed) for v in extra],
-            out_specs=[pl.BlockSpec((rows, half), m) for m in outs],
+            out_specs=[pl.BlockSpec((shape[0], half), m) for m in outs],
         ),
         out_shape=[pltpu.HBM(shape, BF16) for m in outs],
         compiler_params=pltpu.CompilerParams(dimension_semantics=("arbitrary",), vmem_limit_bytes=24 << 20),
@@ -650,7 +655,7 @@
         cost_estimate=SMALL)()
 
 
-def deal_kernel(x_ref, cot_ref, order_ref, gain_ref, me_ref, sendx_ref, sendc_ref, pick_ref, place_ref):
+def deal_kernel(x_ref, cot_ref, order_ref, gain_ref, me_ref, pick_ref, place_ref, *sends):
     rows = x_ref.shape[0]
     dp_size = order_ref.shape[0]
     me = me_ref[0]
@@ -681,27 +686,27 @@
     x = x_ref[...].astype(F32)
     rinv = lax.rsqrt(jnp.mean(x * x, axis=1, keepdims=True) + EPSILON)
     normed = (x * rinv * gain_ref[...]).astype(BF16)
-    sendx_ref[...] = mm(pick, normed).astype(BF16)
-    sendc_ref[...] = mm(pick, cot_ref[...]).astype(BF16)
+    for d in range(dp_size):
+        at = slice(d * pair, (d + 1) * pair)
+        sends[d][...] = mm(pick[at], normed).astype(BF16)
+        sends[dp_size + d][...] = mm(pick[at], cot_ref[...]).astype(BF16)
 
 
 def deal(x, cot, order, gain, me):
     rows, width = x.shape
+    dp_size = order.shape[0]
     vm = pl.BlockSpec(memory_space=pltpu.VMEM)
-    return pl.pallas_call(
+    pick, place, *sends = pl.pallas_call(
         deal_kernel,
         name="deal",
         in_specs=[vm, vm, vm, vm, pl.BlockSpec(memory_space=pltpu.SMEM)],
-        out_specs=[vm] * 4,
-        out_shape=[
-            jax.ShapeDtypeStruct((rows, width), BF16),
-            jax.ShapeDtypeStruct((rows, width), BF16),
-            jax.ShapeDtypeStruct((rows, rows), BF16),
-            jax.ShapeDtypeStruct((rows, rows), BF16),
-        ],
+        out_specs=[vm] * (2 + 2 * dp_size),
+        out_shape=[jax.ShapeDtypeStruct((rows, rows), BF16)] * 2
+        + [jax.ShapeDtypeStruct((rows // dp_size, width), BF16)] * (2 * dp_size),
         compiler_params=pltpu.CompilerParams(vmem_limit_bytes=32 << 20),
         cost_estimate=SMALL,
     )(x, cot, order, gain, me)
+    return sends[:dp_size], sends[dp_size:], pick, place
 
 
 def round_dot(a, b, dims=(((1,), (0,)), ((), ()))):
@@ -792,7 +797,7 @@
     return distances + [half], shards, halves
 
 
-def ring_reduce(ring, grads, terms, weight, place, between):
+def ring_reduce(ring, grads, terms, weight, place, pieces, between):
     half, size = ring.size // 2, ring.size
     step = functools.partial(ring_step, table=ring.at, grads=grads, terms=terms, weight=weight)
     ahead, behind = step(far_kernel, distances=[half])
@@ -800,7 +805,7 @@
         ahead, behind = between(half - d, ahead, ring.hop(ahead, True), ring.hop(behind, False))
         if d > 1:
             ahead, behind = step(pair_kernel, distances=[d - 1, size + 1 - d], arrived=[ahead, behind])
-    return step(own_kernel, distances=[0], arrived=[ahead, behind], place=place)[0]
+    return step(own_kernel, distances=[0], arrived=[ahead, behind], place=place, pieces=pieces)
 
 
 def shards(
@@ -818,8 +823,8 @@
     head = share(jnp.concatenate([deal_order.astype(F32), norm_gain.astype(F32)]), "dp")
     gain_values = in_order(head[:, rows_dev:], "dp").reshape(1, -1)
     send_rows, send_cot, pick, place = deal(block_input, out_cotangent, head[:, :rows_dev], gain_values, me)
-    in_cat = jnp.swapaxes(after(in_weight, send_rows), 0, 1).reshape(in_weight.shape[1], -1)
-    recv_rows = exchange(send_rows.reshape(dp_size, pair, -1), "dp")
+    in_cat = jnp.swapaxes(after(in_weight, send_rows[0]), 0, 1).reshape(in_weight.shape[1], -1)
+    recv_rows = exchange(send_rows, "dp")
     recv_rows, in_cat = lax.optimization_barrier((recv_rows, in_cat))
     in_full = lax.all_gather(in_cat, "dp", axis=0, tiled=True)
     normed = round_dot(place, recv_rows.reshape(rows_dev, -1), TN)
@@ -851,7 +856,7 @@
         elif d < half - 1:
             ahead, behind = bag.meet((ahead, behind), "own", "select", "cot")
             if d == 2:
-                bag["cot"] = exchange(bag["cot"].reshape(dp_size, pair, -1), "dp")
+                bag["cot"] = exchange(bag["cot"], "dp")
         elif d >= half - 1:
             bag["projected"] = placed_product(
                 ring.at, waiting["distances"], waiting["shards"], in_full, NN, bag["projected"])
@@ -886,7 +891,7 @@
     decay_rate = -jnp.exp(decay_full.astype(F32))
     total = jnp.sum(arrived.astype(F32), axis=0).astype(BF16)
     pack_all = swap(jnp.broadcast_to(total[None], part.shape), "tensor")
-    pre, y, gated, hist, unused_state = scan_forward(
+    step_size, slope, y, gated, hist, unused_state = scan_forward(
         here, pack_all, activated, projected, offset, delta_full, delta_shift, decay_rate, skip_values,
         jnp.zeros((states, channels), F32), [], 0, tensor_size)
     gg = mm(group_cot, out_full, NT)
@@ -898,25 +903,27 @@
     ]
     mixed = lax.psum_scatter(round_dot(gated, out_full), "tensor", scatter_dimension=0, tiled=True)
     grad_projected, grad_act, grad_part, unused_carry, rate_grad, delta_weight_grad, row_grads = scan_backward(
-        here, pack_all, pre, activated, projected, gg, y, offset, hist, delta_full, decay_rate, skip_values,
+        here, pack_all, step_size, slope, activated, projected, gg, y, offset, hist, delta_full, decay_rate, skip_values,
         held, [], tensor_size - 1, tensor_size)
     decay_grad = rate_grad * decay_rate
     def by_lane(values):
         lanes = values.reshape(-1, channels // lane_width, dp_size, lane_width // dp_size)
         return jnp.moveaxis(lanes, 2, 0).reshape(dp_size, -1)
 
-    def pack_small(taps_sum, low_sum, bc_sum, row_grads, decay_grad, delta_weight_grad):
+    def pack_scan(row_grads, decay_grad, delta_weight_grad):
+        parts = [by_lane(row_grads[:2]), decay_grad.reshape(dp_size, -1), delta_weight_grad.reshape(dp_size, -1)]
+        return jnp.concatenate(parts, axis=1).astype(BF16), [part.shape[1] for part in parts]
+
+    def pack_conv(packed, taps_sum, low_sum, bc_sum):
         select_grad = jnp.concatenate([low_sum, bc_sum.T], axis=1)
         parts = [
-            by_lane(jnp.concatenate([taps_sum[:taps + 1], row_grads[:2]])),
-            decay_grad.reshape(dp_size, -1),
-            delta_weight_grad.reshape(dp_size, -1),
-            jnp.moveaxis(select_grad.reshape(channels // lane_width, dp_size, -1), 1, 0).reshape(dp_size, -1),
+            packed,
+            by_lane(taps_sum[:taps + 1]).astype(BF16),
+            jnp.moveaxis(select_grad.reshape(channels // lane_width, dp_size, -1), 1, 0).reshape(dp_size, -1).astype(BF16),
         ]
         flat = jnp.concatenate(parts, axis=1)
-        fill = -flat.shape[1] % 2048
-        flat = jnp.pad(flat, ((0, 0), (0, fill))).astype(BF16).reshape(dp_size, -1, LANES)
-        return flat, [part.shape[1] for part in parts]
+        flat = jnp.pad(flat, ((0, 0), (0, -flat.shape[1] % 2048))).reshape(dp_size, -1, LANES)
+        return flat, [part.shape[1] for part in parts[1:]]
 
     merged = channels == width // dp_size
     bag["out"] = weight_grad(
@@ -926,15 +933,16 @@
     bag["gate"] = weight_grad(
         ring.at, distances, normed_shards, after(grad_projected, grad_total), 1, channels, dp_size, False,
         *((2, 1, [bag["out"]]) if merged else ()))
+    bag["packed"], sizes = pack_scan(*(after(v, grad_total) for v in (row_grads, decay_grad, delta_weight_grad)))
     bag["terms"] = round_dot(after(grad_projected, grad_total)[:, channels:], in_full[:, channels:], NT)
-    grad_pack = bag.meet(swap(jnp.broadcast_to(grad_total[None], grad_part.shape), "tensor"), "gate", "terms")
+    grad_pack = bag.meet(swap(jnp.broadcast_to(grad_total[None], grad_part.shape), "tensor"), "gate", "terms", "packed")
     gate_terms = bag["terms"]
     bag["gate"] = lax.psum_scatter(bag["gate"], "dp", scatter_dimension=0, tiled=True)
     if not merged:
         bag["out"] = lax.psum_scatter(bag["out"], "dp", scatter_dimension=0, tiled=True)
     grad_projected, *sums = end(
         here, grad_pack, grad_act, activated, projected, offset, conv_taps, conv_shift, low_w, bc_w, grad_projected)
-    bag["sums"] = [*sums, row_grads, decay_grad, delta_weight_grad]
+    bag["sums"] = [bag["packed"], *sums]
     bag["mixed"] = mixed
 
     def during_grad(k, sent, ahead, behind):
@@ -943,36 +951,39 @@
             bag["grads"] = grad_projected
             names = ["mixed", "sums", "grads"]
         if k == 1:
-            bag["inner"] = weight_grad(ring.at, distances, normed_shards, bag["grads"], 0, channels, dp_size, False)
-            bag["mixed"] = round_dot(place, bag["mixed"])
+            bag["inner"] = weight_grad(
+                ring.at, distances, normed_shards, after(bag["grads"], sent), 0, channels, dp_size, False)
             names = ["mixed", "sums", "inner"]
         if k == half - 2:
+            flat, more = pack_conv(*after(tuple(bag["sums"]), sent))
+            sizes.extend(more)
+            bag["flat"] = swap(flat, "dp")
             names = ["mixed", "flat", "gate"] + ([] if merged else ["out"])
-        if k == half - 1:
-            gate_grad = bag["gate"][:, channels:] if merged else bag["gate"]
-            bag["in"] = jnp.concatenate([bag["inner"], gate_grad]).astype(F32)
-            bag["gain"] = cube_sum(jnp.sum(in_weight.astype(F32) * bag["in"], axis=(0, 2)), "tensor", 1, 2)
-            names = ["gain", "in"]
         ahead, behind = bag.meet((ahead, behind), *names)
+        if k == half - 2:
+            bag["mixed"] = exchange(round_dot(place, bag["mixed"]).reshape(dp_size, pair, -1), "dp")
         if k == 1:
             bag["inner"] = lax.psum_scatter(bag["inner"], "dp", scatter_dimension=0, tiled=True)
-            bag["mixed"] = exchange(bag["mixed"].reshape(dp_size, pair, -1), "dp")
-            flat, waiting["sizes"] = pack_small(*bag["sums"])
-            bag["flat"] = swap(flat, "dp")
         return ahead, behind
 
-    send_grad = ring_reduce(ring, grad_projected, gate_terms, in_full, place, during_grad)
-    home_grad = exchange(send_grad.reshape(dp_size, pair, -1), "dp").reshape(rows_dev, -1)
+    send_grad = ring_reduce(ring, grad_projected, gate_terms, in_full, place, dp_size, during_grad)
+    home_grad = exchange(send_grad, "dp").reshape(rows_dev, -1)
     home_out = bag["mixed"].reshape(rows_dev, -1)
     out_grad = (bag["gate"][0, :channels] if merged else bag["out"][0]).astype(F32)
+    gate_grad = bag["gate"][:, channels:] if merged else bag["gate"]
+    inner_grad = after(bag["inner"], send_grad[0])
+    bag["in"] = jnp.concatenate([inner_grad, gate_grad]).astype(F32)
+    gain_part = jnp.sum(in_weight.astype(F32) * bag["in"], axis=(0, 2))
     in_weight_grad = bag["in"]
-    gain_grad = cube_sum(after(bag["gain"], send_grad), "tensor", 2, tensor_size) / norm_gain.astype(F32)
+    gain_parts = swap(jnp.broadcast_to(gain_part.reshape(1, -1, LANES), (tensor_size, gain_part.size // LANES, LANES)), "tensor")
+    gain_grad = add_up(gain_parts).reshape(-1) / norm_gain.astype(F32)
     flat = jnp.sum(bag["flat"].astype(F32), axis=0).reshape(-1)
     small, start = [], 0
-    for size in waiting["sizes"]:
+    for size in sizes:
         small.append(flat[start:start + size])
         start += size
-    lane_grads = small[0].reshape((taps + 3,) + conv_bias.shape)
+    scan_grads = small[0].reshape((2,) + conv_bias.shape)
+    lane_grads = small[3].reshape((taps + 1,) + conv_bias.shape)
     rows_float = block_input.astype(F32)
     block_output = (rows_float + mm(pick, home_out, TN)).astype(BF16)
     inverse_rms = lax.rsqrt(jnp.mean(rows_float * rows_float, axis=1, keepdims=True) + EPSILON)
@@ -989,11 +1000,11 @@
         in_weight_grad,
         lane_grads[:taps],
         lane_grads[taps],
-        small[3].reshape(select_weight.shape),
+        small[4].reshape(select_weight.shape),
         small[2].reshape(delta_weight.shape),
-        lane_grads[taps + 2],
+        scan_grads[1],
         small[1].reshape(decay_log.shape[1], decay_log.shape[0]).T,
-        lane_grads[taps + 1],
+        scan_grads[0],
         out_grad,
     )
 

time: 490 us -> 485 us (0.990)
  waiting for transfers between devices: 164 us -> 152 us
  starting transfers between devices: 51.4 us -> 58.8 us
    ppermute x21 -> x18, waiting for transfers between devices: 44.3 us -> 33.1 us  [flip(): lax.ppermute(value, axis, [(i, i ^ bit) for i in range(lax.axis_size(axis...]
    all_to_all x5 -> x6, starting transfers between devices: 19.1 us -> 25.2 us  [swap(): return lax.all_to_all(values, axis, split_axis=0, concat_axis=0, tiled=True)]
    all_to_all x5 -> x6, waiting for transfers between devices: 60.2 us -> 65.9 us  [swap(): return lax.all_to_all(values, axis, split_axis=0, concat_axis=0, tiled=True)]
    ppermute x21 -> x18, starting transfers between devices: 15.2 us -> 12.5 us  [flip(): lax.ppermute(value, axis, [(i, i ^ bit) for i in range(lax.axis_size(axis...]
  transfers between devices with their start and end apart: 48 -> 46, of which waited for: 31 -> 30; matrix products, arithmetic and copies ran while one was open for 11% -> 10% of each run, Pallas kernels for 37% -> 38%
where the time goes in v1:
time: 485 us; the launch traced here: 476 us
  Pallas kernels  183 us (38%)
  waiting for transfers between devices  152 us (31%)
  starting transfers between devices  58.8 us (12%)
  matrix products  28.8 us (6%)
  local copies, waits for them, and re-layouts  18.5 us (4%)
  between operations  15.4 us (3%)
  other arithmetic  14.5 us (3%)
  blocking collectives  5.52 us (1%)
    all_to_all x6, waiting for transfers between devices, swap(): return lax.all_to_all(values, axis, split_axis=0, concat_axis=0, tiled=True)  65.9 us
    pallas_call x1, Pallas kernels, scan_backward(): pl.pallas_call(functools.partial(backward_kernel, len(whole)), name='scan...  59.6 us
    ppermute x16, waiting for transfers between devices, hop(): lax.ppermute(value, self.axis, self.forward if ahead else self.backward)  50.6 us
    ppermute x18, waiting for transfers between devices, flip(): lax.ppermute(value, axis, [(i, i ^ bit) for i in range(lax.axis_size(axis...  33.1 us
    dot_general x8, matrix products, mm(): return lax.dot_general(a, b, dims, preferred_element_type=F32)  28.8 us
    pallas_call x1, Pallas kernels, scan_forward(): pl.pallas_call(functools.partial(forward_kernel, len(whole)), name='scan_...  27 us
    pallas_call x3, Pallas kernels, weight_grad(): pl.pallas_call(functools.partial(weight_grad_kernel, count, turned), name...  26.1 us
    all_to_all x6, starting transfers between devices, swap(): return lax.all_to_all(values, axis, split_axis=0, concat_axis=0, tiled=True)  25.2 us
  transfers between devices with their start and end apart: 46, of which 30 were waited for; matrix products, arithmetic and copies ran while one was open for 10% of the time, Pallas kernels for 38%

profile of v1, /device:TPU:0, one launch (start us, length us, event | category | flops | bytes accessed | tf_op | source)
XLA Modules:
  0.0 476.0 jit_solution(12015191545229374807)
XLA Ops:
  34.8 17.4 %collective-permute-done.7.refs_2_ = bf16[192,2048]{1,0:T(8,128)(2,1)S(1)} collective-permute-done((bf16[192,2048]{1,0:T(8,128)(2,1)S(1)}, bf16[192,2048]{1,0:T(8,128)(2,1)S(1)}, u32[]{:S(2)}, u32[]{:S(2)}) %collective-permute-start.7) | collective-permute-done | bytes 786464 | tf_op jit(solution)/shard_map/ppermute | solution.py:784
  64.0 8.5 %collective-permute-done.8.refs_3_ = bf16[192,2048]{1,0:T(8,128)(2,1)S(1)} collective-permute-done((bf16[192,2048]{1,0:T(8,128)(2,1)}, bf16[192,2048]{1,0:T(8,128)(2,1)S(1)}, u32[]{:S(2)}, u32[]{:S(2)}) %collective-permute-start.8) | collective-permute-done | bytes 786464 | tf_op jit(solution)/shard_map/ppermute | solution.py:784
  78.2 11.8 %placed_product.2.refs_3_ = bf16[1536,1024]{1,0:T(8,128)(2,1)} custom-call(s32[8]{0:T(128)S(1)} %dynamic-slice_bitcast_fusion.table_ref, bf16[192,2048]{1,0:T(8,128)(2,1)} %copy-done.4, bf16[192,2048]{1,0:T(8,128)(2,1)} %collective-permute-done.6.refs_1_, bf16[192,2048]{1,0:T(8,128)(2,1)} %copy-done.6, ...), custom_call_target="tpu_custom_call", output_to_operand_aliasing={{}: (7, {})} | custom-call | flops 1 | bytes 1 | tf_op jit(solution)/shard_map/placed_product/pallas_call | solution.py:524
  97.0 6.8 %placed_product.3.refs_8_ = bf16[1536,1024]{1,0:T(8,128)(2,1)} custom-call(s32[8]{0:T(128)S(1)} %dynamic-slice_bitcast_fusion.table_ref, bf16[192,2048]{1,0:T(8,128)(2,1)} %copy-done.5, bf16[192,2048]{1,0:T(8,128)(2,1)} %collective-permute-done.14.refs_1_.refs_6_, ...), custom_call_target="tpu_custom_call", output_to_operand_aliasing={{}: (4, {})} | custom-call | flops 1 | bytes 1 | tf_op jit(solution)/shard_map/placed_product/pallas_call | solution.py:524
  111.3 7.9 %front.1 = (bf16[1536,512]{1,0:T(8,128)(2,1)}, bf16[8,240,128]{2,1,0:T(8,128)(2,1)}) custom-call(s32[1]{0:T(128)} %constant.78.clone.1.me_ref, bf16[1536,1024]{1,0:T(8,128)(2,1)} %placed_halves.1.inner_ref.gate_ref.prior_ref, s32[1536,1]{1,0:T(8,128)S(1)} %reshape_subtract_fusion.offset_ref, f32[4,512]{1,0:T(4,128)S(1)} %slice.188.taps_ref, ...), custom_call_target="tpu_custom_call" | custom-call | flops 1 | bytes 1 | tf_op jit(solution)/shard_map/front/pallas_call | solution.py:87
  131.4 19.5 %all-to-all-done = bf16[8,240,128]{2,1,0:T(8,128)(2,1)S(1)} async-done(((bf16[8,240,128]{2,1,0:T(8,128)(2,1)}), bf16[8,240,128]{2,1,0:T(8,128)(2,1)S(1)}, u32[]{:S(2)}, u32[]{:S(2)}) %all-to-all-start) | async-done | bytes 491552 | tf_op jit(solution)/shard_map/all_to_all | solution.py:730
  155.6 25.2 %all-to-all-done.1.pack_ref = bf16[8,240,128]{2,1,0:T(8,128)(2,1)S(1)} async-done(((bf16[8,240,128]{2,1,0:T(8,128)(2,1)}), bf16[8,240,128]{2,1,0:T(8,128)(2,1)S(1)}, u32[]{:S(2)}, u32[]{:S(2)}) %all-to-all-start.1) | async-done | bytes 491552 | tf_op jit(solution)/shard_map/all_to_all | solution.py:730
  180.8 27.0 %scan_forward.1 = (f32[1536,512]{1,0:T(8,128)}, f32[1536,512]{1,0:T(8,128)}, f32[1536,512]{1,0:T(8,128)}, bf16[1536,512]{1,0:T(8,128)(2,1)}, bf16[24576,512]{1,0:T(8,128)(2,1)}, /*index=5*/f32[16,512]{1,0:T(8,128)}) custom-call(s32[1]{0:T(128)} %constant.78.clone.1.me_ref, bf16[8,240,128]{2,1,0:T(8,128)(2,1)S(1)} %all-to-all-done.1.pack_ref, ...), custom_call_target="tpu_custom_call" | custom-call | flops 1 | bytes 1 | tf_op jit(solution)/shard_map/scan_forward/pallas_call | solution.py:185
  207.8 8.2 %convolution_convert_fusion = bf16[1536,2048]{1,0:T(8,128)(2,1)} fusion(bf16[1536,512]{1,0:T(8,128)(2,1)} %get-tuple-element.164.refs_1_, bf16[512,2048]{1,0:T(8,128)(2,1)} %all-gather.10.cloned.1.call-done), kind=kOutput, calls=%fused_computation | convolution fusion | flops 3224371200 | bytes 9961472 | tf_op jit(solution)/shard_map/dot_general | solution.py:31
  218.3 8.5 %fusion.25.gg_ref = f32[1536,512]{1,0:T(8,128)} fusion(bf16[1536,2048]{1,0:T(8,128)(2,1)} %all-gather.8.cloned.1.call-done.refs_0_, bf16[512,2048]{1,0:T(8,128)(2,1)} %all-gather.10.cloned.1.call-done), kind=kOutput, calls=%fused_computation.91 | convolution fusion | flops 3221225472 | bytes 11534336 | tf_op jit(solution)/shard_map/dot_general | solution.py:31
  226.9 59.6 %scan_backward.1 = (bf16[1536,1024]{1,0:T(8,128)(2,1)}, f32[1536,512]{1,0:T(8,128)}, bf16[8,240,128]{2,1,0:T(8,128)(2,1)}, f32[16,512]{1,0:T(8,128)}, f32[16,512...) custom-call(s32[1]{0:T(128)} %constant.78.clone.1.me_ref, ...), custom_call_target="tpu_custom_call" | custom-call | flops 1 | bytes 1 | tf_op jit(solution)/shard_map/scan_backward/pallas_call | solution.py:330
  290.5 8.5 %weight_grad.3.refs_16_ = bf16[4,1024,512]{2,1,0:T(8,128)(2,1)} custom-call(s32[8]{0:T(128)S(1)} %dynamic-slice_bitcast_fusion.table_ref, bf16[1536,2048]{1,0:T(8,128)(2,1)} %all-gather.8.cloned.1.call-done.refs_0_, bf16[1536,512]{1,0:T(8,128)(2,1)} %get-tuple-element.164.refs_1_), custom_call_target="tpu_custom_call" | custom-call | flops 1 | bytes 1 | tf_op jit(solution)/shard_map/weight_grad/pallas_call | solution.py:479
  309.6 8.8 %weight_grad.4 = bf16[4,1024,512]{2,1,0:T(8,128)(2,1)} custom-call(s32[8]{0:T(128)S(1)} %dynamic-slice_bitcast_fusion.table_ref, bf16[192,2048]{1,0:T(8,128)(2,1)} %copy-done.4, bf16[192,2048]{1,0:T(8,128)(2,1)} %collective-permute-done.6.refs_1_, bf16[192,2048]{1,0:T(8,128)(2,1)} %copy-done.6, ...), custom_call_target="tpu_custom_call", output_to_operand_aliasing={{}: (17, {})} | custom-call | flops 1 | bytes 1 | tf_op jit(solution)/shard_map/weight_grad/pallas_call | solution.py:479
  318.3 8.2 %convolution_convert_fusion.1.t_ref.ta_ref.tb_ref = bf16[1536,2048]{1,0:T(8,128)(2,1)} fusion(bf16[2048,1024]{1,0:T(8,128)(2,1)} %all-gather.6.cloned.1.call-done.refs_5_.refs_2_.refs_0_.refs_1_.refs_3_.refs_4_.refs_6_.refs_7_, bf16[1536,1024]{1,0:T(8,128)(2,1)} %get-tuple-element.168.refs_8_.refs_9_.refs_10_.refs_11_.refs_12_.refs_13_.refs_14_.refs_15_.grad_ref), kind=kOutput, calls=%fused_computation.1 | convolution fusion | flops 3224371200 | bytes 9961472 | tf_op jit(solution)/shard_map/dot_general | solution.py:31
  326.5 5.7 %all-to-all-done.3.pack_ref = bf16[8,240,128]{2,1,0:T(8,128)(2,1)S(1)} async-done(((bf16[8,240,128]{2,1,0:T(8,128)(2,1)}), bf16[8,240,128]{2,1,0:T(8,128)(2,1)S(1)}, u32[]{:S(2)}, u32[]{:S(2)}) %all-to-all-start.3) | async-done | bytes 491552 | tf_op jit(solution)/shard_map/all_to_all | solution.py:730
  332.3 11.3 %end.1 = (bf16[1536,1024]{1,0:T(8,128)(2,1)}, f32[8,512]{1,0:T(8,128)S(1)}, f32[512,128]{1,0:T(8,128)S(1)}, f32[32,512]{1,0:T(8,128)S(1)}) custom-call(s32[1]{0:T(128)} %constant.78.clone.1.me_ref, bf16[8,240,128]{2,1,0:T(8,128)(2,1)S(1)} %all-to-all-done.3.pack_ref, f32[1536,512]{1,0:T(8,128)} %get-tuple-element.177.gact_ref, ...), custom_call_target="tpu_custom_call", output_to_operand_aliasing={{0}: (11, {})} | custom-call | flops 1 | bytes 1 | tf_op jit(solution)/shard_map/end/pallas_call | solution.py:411
  351.0 5.6 %collective-permute-done.20.refs_4_ = bf16[192,1024]{1,0:T(8,128)(2,1)S(1)} collective-permute-done((bf16[192,1024]{1,0:T(8,128)(2,1)}, bf16[192,1024]{1,0:T(8,128)(2,1)S(1)}, u32[]{:S(2)}, u32[]{:S(2)}) %collective-permute-start.20) | collective-permute-done | bytes 393248 | tf_op jit(solution)/shard_map/ppermute | solution.py:784
  366.8 8.9 %weight_grad.5 = bf16[4,512,512]{2,1,0:T(8,128)(2,1)} custom-call(s32[8]{0:T(128)S(1)} %dynamic-slice_bitcast_fusion.table_ref, bf16[192,2048]{1,0:T(8,128)(2,1)} %copy-done.4, bf16[192,2048]{1,0:T(8,128)(2,1)} %collective-permute-done.6.refs_1_, bf16[192,2048]{1,0:T(8,128)(2,1)} %copy-done.6, bf16[192,2048]{1,0:T(8,128)(2,1)} %copy-done.7, ...), custom_call_target="tpu_custom_call" | custom-call | flops 1 | bytes 1 | tf_op jit(solution)/shard_map/weight_grad/pallas_call | solution.py:479
  375.7 5.6 %collective-permute-done.23.refs_5_ = bf16[192,2048]{1,0:T(8,128)(2,1)S(1)} collective-permute-done((bf16[192,2048]{1,0:T(8,128)(2,1)}, bf16[192,2048]{1,0:T(8,128)(2,1)S(1)}, u32[]{:S(2)}, u32[]{:S(2)}) %collective-permute-start.23) | collective-permute-done | bytes 786464 | tf_op jit(solution)/shard_map/ppermute | solution.py:784
  398.3 6.5 %all-to-all-done.4 = bf16[4,320,128]{2,1,0:T(8,128)(2,1)S(1)} async-done(((bf16[4,320,128]{2,1,0:T(8,128)(2,1)}), bf16[4,320,128]{2,1,0:T(8,128)(2,1)S(1)}, u32[]{:S(2)}, u32[]{:S(2)}) %all-to-all-start.4) | async-done | bytes 327712 | tf_op jit(solution)/shard_map/all_to_all | solution.py:730
  404.8 5.6 %collective-permute-done.25.refs_5_ = bf16[192,2048]{1,0:T(8,128)(2,1)} collective-permute-done((bf16[192,2048]{1,0:T(8,128)(2,1)}, bf16[192,2048]{1,0:T(8,128)(2,1)}, u32[]{:S(2)}, u32[]{:S(2)}) %collective-permute-start.25) | collective-permute-done | bytes 786464 | tf_op jit(solution)/shard_map/ppermute | solution.py:784
  425.6 7.6 %collective-permute-done.28 = bf16[48,2048]{1,0:T(8,128)(2,1)S(1)} collective-permute-done((bf16[48,2048]{1,0:T(8,128)(2,1)S(1)}, bf16[48,2048]{1,0:T(8,128)(2,1)S(1)}, u32[]{:S(2)}, u32[]{:S(2)}) %collective-permute-start.28) | collective-permute-done | bytes 196640 | tf_op jit(solution)/shard_map/ppermute | solution.py:721
  438.8 6.1 %own_kernel.1 = (bf16[48,2048]{1,0:T(8,128)(2,1)}, bf16[48,2048]{1,0:T(8,128)(2,1)}, bf16[48,2048]{1,0:T(8,128)(2,1)}, bf16[48,2048]{1,0:T(8,128)(2,1)}) custom-call(s32[8]{0:T(128)S(1)} %dynamic-slice_bitcast_fusion.table_ref, bf16[1536,1024]{1,0:T(8,128)(2,1)} %get-tuple-element.191.g_ref.ga_ref.gb_ref.refs_8_.refs_9_.refs_10_.refs_11_.refs_12_.refs_13_.refs_14_.refs_15_, ...), custom_call_target="tpu_custom_call" | custom-call | flops 1 | bytes 1 | tf_op jit(solution)/shard_map/own_kernel/pallas_call | solution.py:630
  448.2 5.7 %all-to-all-start.5 = ((f32[8,4,128]{2,1,0:T(4,128)}), f32[8,4,128]{2,1,0:T(4,128)S(1)}, u32[]{:S(2)}, u32[]{:S(2)}) async-start(f32[8,4,128]{2,1,0:T(4,128)} %broadcast_in_dim.53), calls=%async_computation.8 | async-start | bytes 32768 | tf_op jit(solution)/shard_map/all_to_all | solution.py:730
  (289 shorter events, 166.1 us)
Async XLA Ops:
  7.2 71.0 %all-gather.6.cloned.1.call-start = ((), (), s32[]{:S(2)}) async-start(), calls=%async_computation.9 | async-start | bytes 5242880 | tf_op jit(solution)/shard_map/all_gather | solution.py:829
  32.1 175.8 %all-gather.10.cloned.1.call-start = ((), (), s32[]{:S(2)}) async-start(), calls=%async_computation.11 | async-start | bytes 2621440 | tf_op jit(solution)/shard_map/all_gather | solution.py:883
  32.5 19.8 %collective-permute-start.7 = (bf16[192,2048]{1,0:T(8,128)(2,1)S(1)}, bf16[192,2048]{1,0:T(8,128)(2,1)S(1)}, u32[]{:S(2)}, u32[]{:S(2)}) collective-permute-start(bf16[192,2048]{1,0:T(8,128)(2,1)S(1)} %convolution_convert_fusion.4.refs_0_), channel_id=1, source_target_pairs={{1,0},{3,1},{5,3},{7,5},{6,7},{4,6},{2,4},{0,2},{9,8},{11,9},{13,1... | collective-permute-start | bytes 2359304 | tf_op jit(solution)/shard_map/ppermute | solution.py:784
  34.1 19.5 %collective-permute-start.6 = (bf16[192,2048]{1,0:T(8,128)(2,1)S(1)}, bf16[192,2048]{1,0:T(8,128)(2,1)}, u32[]{:S(2)}, u32[]{:S(2)}) collective-permute-start(bf16[192,2048]{1,0:T(8,128)(2,1)S(1)} %convolution_convert_fusion.4.refs_0_), channel_id=1, source_target_pairs={{0,1},{1,3},{3,5},{5,7},{7,6},{6,4},{4,2},{2,0},{8,9},{9,11},{11,1... | collective-permute-start | bytes 2359304 | tf_op jit(solution)/shard_map/ppermute | solution.py:784
  53.7 18.8 %collective-permute-start.8 = (bf16[192,2048]{1,0:T(8,128)(2,1)}, bf16[192,2048]{1,0:T(8,128)(2,1)S(1)}, u32[]{:S(2)}, u32[]{:S(2)}) collective-permute-start(bf16[192,2048]{1,0:T(8,128)(2,1)} %collective-permute-done.6.refs_1_), channel_id=1, source_target_pairs={{0,1},{1,3},{3,5},{5,7},{7,6},{6,4},{4,2},{2,0},{8,9},{9,11},{11,1... | collective-permute-start | bytes 2359304 | tf_op jit(solution)/shard_map/ppermute | solution.py:784
  54.1 18.4 %collective-permute-start.9 = (bf16[192,2048]{1,0:T(8,128)(2,1)S(1)}, bf16[192,2048]{1,0:T(8,128)(2,1)S(1)}, u32[]{:S(2)}, u32[]{:S(2)}) collective-permute-start(bf16[192,2048]{1,0:T(8,128)(2,1)S(1)} %collective-permute-done.7.refs_2_), channel_id=1, source_target_pairs={{1,0},{3,1},{5,3},{7,5},{6,7},{4,6},{2,4},{0,2},{9,8},{11,9},{13,1... | collective-permute-start | bytes 2359304 | tf_op jit(solution)/shard_map/ppermute | solution.py:784
  73.5 144.8 %all-gather.8.cloned.1.call-start = ((), (), s32[]{:S(2)}) async-start(), calls=%async_computation.10 | async-start | bytes 7077888 | tf_op jit(solution)/shard_map/all_gather | solution.py:884
  73.6 17.6 %collective-permute-start.13 = (bf16[192,2048]{1,0:T(8,128)(2,1)S(1)}, bf16[192,2048]{1,0:T(8,128)(2,1)S(1)}, u32[]{:S(2)}, u32[]{:S(2)}) collective-permute-start(bf16[192,2048]{1,0:T(8,128)(2,1)S(1)} %collective-permute-done.8.refs_3_), channel_id=1, source_target_pairs={{0,1},{1,3},{3,5},{5,7},{7,6},{6,4},{4,2},{2,0},{8,9},{9,11},{11,1... | collective-permute-start | bytes 2359304 | tf_op jit(solution)/shard_map/ppermute | solution.py:784
  75.1 17.6 %collective-permute-start.14 = (bf16[192,2048]{1,0:T(8,128)(2,1)}, bf16[192,2048]{1,0:T(8,128)(2,1)}, u32[]{:S(2)}, u32[]{:S(2)}) collective-permute-start(bf16[192,2048]{1,0:T(8,128)(2,1)} %copy-done.8), channel_id=1, source_target_pairs={{1,0},{3,1},{5,3},{7,5},{6,7},{4,6},{2,4},{0,2},{9,8},{11,9},{13,1... | collective-permute-start | bytes 2359304 | tf_op jit(solution)/shard_map/ppermute | solution.py:784
  75.6 20.2 %collective-permute-start.17 = (bf16[48,2048]{1,0:T(8,128)(2,1)S(1)}, bf16[48,2048]{1,0:T(8,128)(2,1)S(1)}, u32[]{:S(2)}, u32[]{:S(2)}) collective-permute-start(bf16[48,2048]{1,0:T(8,128)(2,1)S(1)} %get-tuple-element.140), channel_id=1, source_target_pairs={{0,8},{8,0},{16,24},{24,16},{1,9},{9,1},{17,25},{25,17},{2,10},{10... | collective-permute-start | bytes 589832 | tf_op jit(solution)/shard_map/ppermute | solution.py:721
  75.7 20.2 %collective-permute-start.18 = (bf16[48,2048]{1,0:T(8,128)(2,1)S(1)}, bf16[48,2048]{1,0:T(8,128)(2,1)}, u32[]{:S(2)}, u32[]{:S(2)}) collective-permute-start(bf16[48,2048]{1,0:T(8,128)(2,1)S(1)} %get-tuple-element.141), channel_id=1, source_target_pairs={{0,16},{8,24},{16,0},{24,8},{1,17},{9,25},{17,1},{25,9},{2,18},{10... | collective-permute-start | bytes 589832 | tf_op jit(solution)/shard_map/ppermute | solution.py:721
  76.3 19.6 %collective-permute-start.19 = (bf16[48,2048]{1,0:T(8,128)(2,1)S(1)}, bf16[48,2048]{1,0:T(8,128)(2,1)}, u32[]{:S(2)}, u32[]{:S(2)}) collective-permute-start(bf16[48,2048]{1,0:T(8,128)(2,1)S(1)} %get-tuple-element.142), channel_id=1, source_target_pairs={{0,24},{8,16},{16,8},{24,0},{1,25},{9,17},{17,9},{25,1},{2,26},{10... | collective-permute-start | bytes 589832 | tf_op jit(solution)/shard_map/ppermute | solution.py:721
  119.1 31.8 %all-to-all-start = ((bf16[8,240,128]{2,1,0:T(8,128)(2,1)}), bf16[8,240,128]{2,1,0:T(8,128)(2,1)S(1)}, u32[]{:S(2)}, u32[]{:S(2)}) async-start(bf16[8,240,128]{2,1,0:T(8,128)(2,1)} %get-tuple-element.148), calls=%async_computation | async-start | bytes 983040 | tf_op jit(solution)/shard_map/all_to_all | solution.py:730
  151.8 29.0 %all-to-all-start.1 = ((bf16[8,240,128]{2,1,0:T(8,128)(2,1)}), bf16[8,240,128]{2,1,0:T(8,128)(2,1)S(1)}, u32[]{:S(2)}, u32[]{:S(2)}) async-start(bf16[8,240,128]{2,1,0:T(8,128)(2,1)} %broadcast_in_dim.26), calls=%async_computation.1 | async-start | bytes 983040 | tf_op jit(solution)/shard_map/all_to_all | solution.py:730
  155.3 203.7 %reduce-scatter.4.cloned.1.call-start = ((), (), s32[]{:S(2)}) async-start(), calls=%async_computation.12 | async-start | bytes 7077888 | tf_op jit(solution)/shard_map/reduce_scatter | solution.py:904
  286.5 18.0 %all-to-all-start.2 = ((bf16[8,240,128]{2,1,0:T(8,128)(2,1)}), bf16[8,240,128]{2,1,0:T(8,128)(2,1)S(1)}, u32[]{:S(2)}, u32[]{:S(2)}) async-start(bf16[8,240,128]{2,1,0:T(8,128)(2,1)} %get-tuple-element.162), calls=%async_computation.2 | async-start | bytes 983040 | tf_op jit(solution)/shard_map/all_to_all | solution.py:730
  305.8 26.5 %all-to-all-start.3 = ((bf16[8,240,128]{2,1,0:T(8,128)(2,1)}), bf16[8,240,128]{2,1,0:T(8,128)(2,1)S(1)}, u32[]{:S(2)}, u32[]{:S(2)}) async-start(bf16[8,240,128]{2,1,0:T(8,128)(2,1)} %broadcast_in_dim.29), calls=%async_computation.3 | async-start | bytes 983040 | tf_op jit(solution)/shard_map/all_to_all | solution.py:730
  309.4 100.9 %reduce-scatter.6.cloned.1.call-start = ((), (), s32[]{:S(2)}) async-start(), calls=%async_computation.13 | async-start | bytes 5242880 | tf_op jit(solution)/shard_map/reduce_scatter | solution.py:940
  332.3 112.7 %reduce-scatter.8.cloned.1.call-start = ((), (), s32[]{:S(2)}) async-start(), calls=%async_computation.14 | async-start | bytes 2621440 | tf_op jit(solution)/shard_map/reduce_scatter | solution.py:966
  364.8 16.5 %collective-permute-start.23 = (bf16[192,2048]{1,0:T(8,128)(2,1)}, bf16[192,2048]{1,0:T(8,128)(2,1)S(1)}, u32[]{:S(2)}, u32[]{:S(2)}) collective-permute-start(bf16[192,2048]{1,0:T(8,128)(2,1)} %get-tuple-element.189), channel_id=1, source_target_pairs={{1,0},{3,1},{5,3},{7,5},{6,7},{4,6},{2,4},{0,2},{9,8},{11,9},{13,1... | collective-permute-start | bytes 2359304 | tf_op jit(solution)/shard_map/ppermute | solution.py:784
  365.2 16.5 %collective-permute-start.22 = (bf16[192,2048]{1,0:T(8,128)(2,1)}, bf16[192,2048]{1,0:T(8,128)(2,1)S(1)}, u32[]{:S(2)}, u32[]{:S(2)}) collective-permute-start(bf16[192,2048]{1,0:T(8,128)(2,1)} %get-tuple-element.188), channel_id=1, source_target_pairs={{0,1},{1,3},{3,5},{5,7},{7,6},{6,4},{4,2},{2,0},{8,9},{9,11},{11,1... | collective-permute-start | bytes 2359304 | tf_op jit(solution)/shard_map/ppermute | solution.py:784
  387.6 22.8 %collective-permute-start.24 = (bf16[192,2048]{1,0:T(8,128)(2,1)}, bf16[192,2048]{1,0:T(8,128)(2,1)}, u32[]{:S(2)}, u32[]{:S(2)}) collective-permute-start(bf16[192,2048]{1,0:T(8,128)(2,1)} %get-tuple-element.199), channel_id=1, source_target_pairs={{0,1},{1,3},{3,5},{5,7},{7,6},{6,4},{4,2},{2,0},{8,9},{9,11},{11,1... | collective-permute-start | bytes 2359304 | tf_op jit(solution)/shard_map/ppermute | solution.py:784
  392.5 17.9 %collective-permute-start.25 = (bf16[192,2048]{1,0:T(8,128)(2,1)}, bf16[192,2048]{1,0:T(8,128)(2,1)}, u32[]{:S(2)}, u32[]{:S(2)}) collective-permute-start(bf16[192,2048]{1,0:T(8,128)(2,1)} %get-tuple-element.200), channel_id=1, source_target_pairs={{1,0},{3,1},{5,3},{7,5},{6,7},{4,6},{2,4},{0,2},{9,8},{11,9},{13,1... | collective-permute-start | bytes 2359304 | tf_op jit(solution)/shard_map/ppermute | solution.py:784
  420.1 17.0 %collective-permute-start.29 = (bf16[192,2048]{1,0:T(8,128)(2,1)}, bf16[192,2048]{1,0:T(8,128)(2,1)S(1)}, u32[]{:S(2)}, u32[]{:S(2)}) collective-permute-start(bf16[192,2048]{1,0:T(8,128)(2,1)} %get-tuple-element.214), channel_id=1, source_target_pairs={{0,1},{1,3},{3,5},{5,7},{7,6},{6,4},{4,2},{2,0},{8,9},{9,11},{11,1... | collective-permute-start | bytes 2359304 | tf_op jit(solution)/shard_map/ppermute | solution.py:784
  (61 other events, 481.1 us)
Sparse Core Ops, SparseCore 0:
  32.2 37.6 all-gather.5
  73.6 26.2 all-gather.9
  105.4 112.8 all-gather.7
  221.8 128.1 reduce-scatter.3
  352.4 42.8 reduce-scatter.5
  398.4 35.2 reduce-scatter.7

commit v2 on v1

--- a/solution.py
+++ b/solution.py
@@ -10,7 +10,7 @@
 EPSILON = 1e-05
 FAR = 1e30
 LANES = 128
-STEP = 48
+STEP = 96
 SPAN = 16
 SMALL = pl.CostEstimate(flops=1, transcendentals=0, bytes_accessed=1)
 NT = (((1,), (1,)), ((), ()))
@@ -277,28 +277,41 @@
             rgrad = rgrad + through * dts[j:j + 1, :]
             at = pl.multiple_of((base + j) * states, states)
             adj_s[pl.ds(at, states), :] = adj.astype(BF16)
-            thr_s[pl.ds(at, states), :] = (through * rate).astype(BF16)
+            scaled = through * rate
+            scaled = scaled[:states // 2] + scaled[states // 2:]
+            if j % 2:
+                later = scaled
+            else:
+                at = pl.multiple_of((base + j) * (states // 2), states)
+                thr_s[pl.ds(at, states), :] = jnp.concatenate([scaled, later], axis=0).astype(BF16)
         return carry, rgrad
 
     carry, rgrad = lax.fori_loop(0, groups, group, (carry_s[...], rgrad_ref[...]))
     carry_s[...] = carry
     rgrad_ref[...] = rgrad
     spread = spread_columns(bt, chunk, states)
-    ones = jnp.where(spread_mask(SPAN, states), 1.0, 0.0).astype(BF16)
     width = SPAN * states
+    ones = (
+        lax.broadcasted_iota(jnp.int32, (2 * SPAN, width), 0)
+        == lax.broadcasted_iota(jnp.int32, (2 * SPAN, width), 1) // (states // 2)
+    ).astype(BF16)
     ub = u_s[...].astype(BF16)
     gyb = gy.astype(BF16)
     ahead = (lax.broadcasted_iota(jnp.int32, (width, chunk), 1)
              - lax.broadcasted_iota(jnp.int32, (width, chunk), 0) // states)
+    gb_wide = mm(adj_s[...], ub, NT)
+    gc_wide = mm(hist_ref[...], gyb, NT)
     gb_all = jnp.zeros((width, chunk), F32)
     gc_all = jnp.zeros((width, chunk), F32)
     for g in range(chunk // SPAN):
         rows = slice(g * SPAN, (g + 1) * SPAN)
         adj = adj_s[g * width:(g + 1) * width, :]
         drive_s[rows, :] = mm(spread[rows, :], adj)
-        decay_s[rows, :] = mm(ones, thr_s[g * width:(g + 1) * width, :])
-        gb_all = jnp.where(ahead == g * SPAN, mm(adj, ub, NT), gb_all)
-        gc_all = jnp.where(ahead == g * SPAN, mm(hist_ref[g * width:(g + 1) * width, :], gyb, NT), gc_all)
+        if g % 2 == 0:
+            pair = slice(g * SPAN, (g + 2) * SPAN)
+            decay_s[pair, :] = mm(ones, thr_s[g * width // 2:(g + 2) * width // 2, :])
+        gb_all = jnp.where(ahead == g * SPAN, gb_wide[g * width:(g + 1) * width], gb_all)
+        gc_all = jnp.where(ahead == g * SPAN, gc_wide[g * width:(g + 1) * width], gc_all)
     tiles = tile_matrix(states)
     wide_s[0:states, 0:chunk] = mm(tiles, gb_all.astype(BF16))
     wide_s[states:2 * states, 0:chunk] = mm(tiles, gc_all.astype(BF16))
@@ -351,11 +364,11 @@
             out_specs=blocks + sums,
             scratch_shapes=[pltpu.VMEM((chunk, channels), F32)] * 5
             + [pltpu.VMEM((2 * states, 2 * LANES), F32)]
-            + [pltpu.VMEM((chunk * states, channels), BF16)] * 2,
+            + [pltpu.VMEM((chunk * states, channels), BF16), pltpu.VMEM((chunk * states // 2, channels), BF16)],
         ),
         out_shape=shapes + [jax.ShapeDtypeStruct(v.shape, F32) for v in held],
         input_output_aliases={18 + i: i for i in range(len(whole))},
-        compiler_params=pltpu.CompilerParams(dimension_semantics=("arbitrary",), vmem_limit_bytes=24 << 20),
+        compiler_params=pltpu.CompilerParams(dimension_semantics=("arbitrary",), vmem_limit_bytes=40 << 20),
         cost_estimate=SMALL,
     )(me, pack, in_hbm(dt), in_hbm(sp), in_hbm(act), in_hbm(projected), in_hbm(gg), in_hbm(y), offset, in_hbm(hist), in_hbm(hist), delta_w, rate, skip, *held, *(in_hbm(v) if k == 1 else v for k, v in enumerate(whole)))
 

time: 485 us -> 478 us (0.986)
  Pallas kernels: 183 us -> 174 us
  waiting for transfers between devices: 152 us -> 157 us
    pallas_call x1, Pallas kernels: 59.6 us -> 52.1 us  [scan_backward(): pl.pallas_call(functools.partial(backward_kernel, len(whole)), name='scan...]
  transfers between devices with their start and end apart: 46 -> 46, of which waited for: 30 -> 28; matrix products, arithmetic and copies ran while one was open for 10% -> 10% of each run, Pallas kernels for 38% -> 37%
where the time goes in v2:
time: 478 us; the launch traced here: 469 us
  Pallas kernels  174 us (36%)
  waiting for transfers between devices  157 us (33%)
  starting transfers between devices  55 us (12%)
  matrix products  28.8 us (6%)
  local copies, waits for them, and re-layouts  19.4 us (4%)
  between operations  15.4 us (3%)
  other arithmetic  14.5 us (3%)
  blocking collectives  5.52 us (1%)
    all_to_all x6, waiting for transfers between devices, swap(): return lax.all_to_all(values, axis, split_axis=0, concat_axis=0, tiled=True)  64.9 us
    pallas_call x1, Pallas kernels, scan_backward(): pl.pallas_call(functools.partial(backward_kernel, len(whole)), name='scan...  52.1 us
    ppermute x16, waiting for transfers between devices, hop(): lax.ppermute(value, self.axis, self.forward if ahead else self.backward)  50.6 us
    ppermute x18, waiting for transfers between devices, flip(): lax.ppermute(value, axis, [(i, i ^ bit) for i in range(lax.axis_size(axis...  37.1 us
    dot_general x8, matrix products, mm(): return lax.dot_general(a, b, dims, preferred_element_type=F32)  28.8 us
    pallas_call x3, Pallas kernels, weight_grad(): pl.pallas_call(functools.partial(weight_grad_kernel, count, turned), name...  26.2 us
    pallas_call x1, Pallas kernels, scan_forward(): pl.pallas_call(functools.partial(forward_kernel, len(whole)), name='scan_...  25.4 us
    pallas_call x5, Pallas kernels, ring_step(): pl.pallas_call(functools.partial(kernel, cuts, halves=True) if small else...  25.1 us
  transfers between devices with their start and end apart: 46, of which 28 were waited for; matrix products, arithmetic and copies ran while one was open for 10% of the time, Pallas kernels for 37%

profile of v2, /device:TPU:0, one launch (start us, length us, event | category | flops | bytes accessed | tf_op | source)
XLA Modules:
  0.0 468.6 jit_solution(9700073350788766794)
XLA Ops:
  34.8 17.4 %collective-permute-done.7.refs_2_ = bf16[192,2048]{1,0:T(8,128)(2,1)S(1)} collective-permute-done((bf16[192,2048]{1,0:T(8,128)(2,1)S(1)}, bf16[192,2048]{1,0:T(8,128)(2,1)S(1)}, u32[]{:S(2)}, u32[]{:S(2)}) %collective-permute-start.7) | collective-permute-done | bytes 786464 | tf_op jit(solution)/shard_map/ppermute | solution.py:797
  64.0 8.5 %collective-permute-done.8.refs_3_ = bf16[192,2048]{1,0:T(8,128)(2,1)S(1)} collective-permute-done((bf16[192,2048]{1,0:T(8,128)(2,1)}, bf16[192,2048]{1,0:T(8,128)(2,1)S(1)}, u32[]{:S(2)}, u32[]{:S(2)}) %collective-permute-start.8) | collective-permute-done | bytes 786464 | tf_op jit(solution)/shard_map/ppermute | solution.py:797
  78.2 11.8 %placed_product.2.refs_3_ = bf16[1536,1024]{1,0:T(8,128)(2,1)} custom-call(s32[8]{0:T(128)S(1)} %dynamic-slice_bitcast_fusion.table_ref, bf16[192,2048]{1,0:T(8,128)(2,1)} %copy-done.4, bf16[192,2048]{1,0:T(8,128)(2,1)} %collective-permute-done.6.refs_1_, bf16[192,2048]{1,0:T(8,128)(2,1)} %copy-done.6, ...), custom_call_target="tpu_custom_call", output_to_operand_aliasing={{}: (7, {})} | custom-call | flops 1 | bytes 1 | tf_op jit(solution)/shard_map/placed_product/pallas_call | solution.py:537
  97.0 6.8 %placed_product.3.refs_8_ = bf16[1536,1024]{1,0:T(8,128)(2,1)} custom-call(s32[8]{0:T(128)S(1)} %dynamic-slice_bitcast_fusion.table_ref, bf16[192,2048]{1,0:T(8,128)(2,1)} %copy-done.5, bf16[192,2048]{1,0:T(8,128)(2,1)} %collective-permute-done.14.refs_1_.refs_6_, ...), custom_call_target="tpu_custom_call", output_to_operand_aliasing={{}: (4, {})} | custom-call | flops 1 | bytes 1 | tf_op jit(solution)/shard_map/placed_product/pallas_call | solution.py:537
  111.3 7.9 %front.1 = (bf16[1536,512]{1,0:T(8,128)(2,1)}, bf16[8,240,128]{2,1,0:T(8,128)(2,1)}) custom-call(s32[1]{0:T(128)} %constant.78.clone.1.me_ref, bf16[1536,1024]{1,0:T(8,128)(2,1)} %placed_halves.1.inner_ref.gate_ref.prior_ref, s32[1536,1]{1,0:T(8,128)S(1)} %reshape_subtract_fusion.offset_ref, f32[4,512]{1,0:T(4,128)S(1)} %slice.188.taps_ref, ...), custom_call_target="tpu_custom_call" | custom-call | flops 1 | bytes 1 | tf_op jit(solution)/shard_map/front/pallas_call | solution.py:87
  123.9 5.5 %all-gather.1 = bf16[4,36,512]{2,1,0:T(8,128)(2,1)S(1)} all-gather(bf16[1,36,512]{2,1,0:T(8,128)(2,1)S(1)} %bitcast.155), channel_id=2, replica_groups=mesh['dp'=4,'tensor'=8] {'dp'}, dimensions={0}, use_global_device_ids=true | all-gather | bytes 184320 | tf_op jit(solution)/shard_map/all_gather | solution.py:898
  131.4 19.5 %all-to-all-done = bf16[8,240,128]{2,1,0:T(8,128)(2,1)S(1)} async-done(((bf16[8,240,128]{2,1,0:T(8,128)(2,1)}), bf16[8,240,128]{2,1,0:T(8,128)(2,1)S(1)}, u32[]{:S(2)}, u32[]{:S(2)}) %all-to-all-start) | async-done | bytes 491552 | tf_op jit(solution)/shard_map/all_to_all | solution.py:743
  155.6 25.2 %all-to-all-done.1.pack_ref = bf16[8,240,128]{2,1,0:T(8,128)(2,1)S(1)} async-done(((bf16[8,240,128]{2,1,0:T(8,128)(2,1)}), bf16[8,240,128]{2,1,0:T(8,128)(2,1)S(1)}, u32[]{:S(2)}, u32[]{:S(2)}) %all-to-all-start.1) | async-done | bytes 491552 | tf_op jit(solution)/shard_map/all_to_all | solution.py:743
  180.8 25.4 %scan_forward.1 = (f32[1536,512]{1,0:T(8,128)}, f32[1536,512]{1,0:T(8,128)}, f32[1536,512]{1,0:T(8,128)}, bf16[1536,512]{1,0:T(8,128)(2,1)}, bf16[24576,512]{1,0:T(8,128)(2,1)}, /*index=5*/f32[16,512]{1,0:T(8,128)}) custom-call(s32[1]{0:T(128)} %constant.78.clone.1.me_ref, bf16[8,240,128]{2,1,0:T(8,128)(2,1)S(1)} %all-to-all-done.1.pack_ref, ...), custom_call_target="tpu_custom_call" | custom-call | flops 1 | bytes 1 | tf_op jit(solution)/shard_map/scan_forward/pallas_call | solution.py:185
  206.3 8.2 %convolution_convert_fusion = bf16[1536,2048]{1,0:T(8,128)(2,1)} fusion(bf16[1536,512]{1,0:T(8,128)(2,1)} %get-tuple-element.164.refs_1_, bf16[512,2048]{1,0:T(8,128)(2,1)} %all-gather.10.cloned.1.call-done), kind=kOutput, calls=%fused_computation | convolution fusion | flops 3224371200 | bytes 9961472 | tf_op jit(solution)/shard_map/dot_general | solution.py:31
  218.3 8.5 %fusion.25.gg_ref = f32[1536,512]{1,0:T(8,128)} fusion(bf16[1536,2048]{1,0:T(8,128)(2,1)} %all-gather.8.cloned.1.call-done.refs_0_, bf16[512,2048]{1,0:T(8,128)(2,1)} %all-gather.10.cloned.1.call-done), kind=kOutput, calls=%fused_computation.91 | convolution fusion | flops 3221225472 | bytes 11534336 | tf_op jit(solution)/shard_map/dot_general | solution.py:31
  226.9 52.1 %scan_backward.1 = (bf16[1536,1024]{1,0:T(8,128)(2,1)}, f32[1536,512]{1,0:T(8,128)}, bf16[8,240,128]{2,1,0:T(8,128)(2,1)}, f32[16,512]{1,0:T(8,128)}, f32[16,512...) custom-call(s32[1]{0:T(128)} %constant.78.clone.1.me_ref, ...), custom_call_target="tpu_custom_call" | custom-call | flops 1 | bytes 1 | tf_op jit(solution)/shard_map/scan_backward/pallas_call | solution.py:343
  283.0 8.5 %weight_grad.3.refs_16_ = bf16[4,1024,512]{2,1,0:T(8,128)(2,1)} custom-call(s32[8]{0:T(128)S(1)} %dynamic-slice_bitcast_fusion.table_ref, bf16[1536,2048]{1,0:T(8,128)(2,1)} %all-gather.8.cloned.1.call-done.refs_0_, bf16[1536,512]{1,0:T(8,128)(2,1)} %get-tuple-element.164.refs_1_), custom_call_target="tpu_custom_call" | custom-call | flops 1 | bytes 1 | tf_op jit(solution)/shard_map/weight_grad/pallas_call | solution.py:492
  291.4 5.4 %all-to-all-done.2 = bf16[8,240,128]{2,1,0:T(8,128)(2,1)S(1)} async-done(((bf16[8,240,128]{2,1,0:T(8,128)(2,1)}), bf16[8,240,128]{2,1,0:T(8,128)(2,1)S(1)}, u32[]{:S(2)}, u32[]{:S(2)}) %all-to-all-start.2) | async-done | bytes 491552 | tf_op jit(solution)/shard_map/all_to_all | solution.py:743
  301.8 8.8 %weight_grad.4 = bf16[4,1024,512]{2,1,0:T(8,128)(2,1)} custom-call(s32[8]{0:T(128)S(1)} %dynamic-slice_bitcast_fusion.table_ref, bf16[192,2048]{1,0:T(8,128)(2,1)} %copy-done.4, bf16[192,2048]{1,0:T(8,128)(2,1)} %collective-permute-done.6.refs_1_, bf16[192,2048]{1,0:T(8,128)(2,1)} %copy-done.6, ...), custom_call_target="tpu_custom_call", output_to_operand_aliasing={{}: (17, {})} | custom-call | flops 1 | bytes 1 | tf_op jit(solution)/shard_map/weight_grad/pallas_call | solution.py:492
  310.6 8.2 %convolution_convert_fusion.1.t_ref.ta_ref.tb_ref = bf16[1536,2048]{1,0:T(8,128)(2,1)} fusion(bf16[2048,1024]{1,0:T(8,128)(2,1)} %all-gather.6.cloned.1.call-done.refs_5_.refs_2_.refs_0_.refs_1_.refs_3_.refs_4_.refs_6_.refs_7_, bf16[1536,1024]{1,0:T(8,128)(2,1)} %get-tuple-element.168.refs_8_.refs_9_.refs_10_.refs_11_.refs_12_.refs_13_.refs_14_.refs_15_.grad_ref), kind=kOutput, calls=%fused_computation.1 | convolution fusion | flops 3224371200 | bytes 9961472 | tf_op jit(solution)/shard_map/dot_general | solution.py:31
  324.0 11.3 %end.1 = (bf16[1536,1024]{1,0:T(8,128)(2,1)}, f32[8,512]{1,0:T(8,128)S(1)}, f32[512,128]{1,0:T(8,128)S(1)}, f32[32,512]{1,0:T(8,128)S(1)}) custom-call(s32[1]{0:T(128)} %constant.78.clone.1.me_ref, bf16[8,240,128]{2,1,0:T(8,128)(2,1)S(1)} %all-to-all-done.3.pack_ref, f32[1536,512]{1,0:T(8,128)} %get-tuple-element.177.gact_ref, ...), custom_call_target="tpu_custom_call", output_to_operand_aliasing={{0}: (11, {})} | custom-call | flops 1 | bytes 1 | tf_op jit(solution)/shard_map/end/pallas_call | solution.py:424
  341.7 6.7 %collective-permute-done.20.refs_4_ = bf16[192,1024]{1,0:T(8,128)(2,1)S(1)} collective-permute-done((bf16[192,1024]{1,0:T(8,128)(2,1)}, bf16[192,1024]{1,0:T(8,128)(2,1)S(1)}, u32[]{:S(2)}, u32[]{:S(2)}) %collective-permute-start.20) | collective-permute-done | bytes 393248 | tf_op jit(solution)/shard_map/ppermute | solution.py:797
  357.1 9.0 %weight_grad.5 = bf16[4,512,512]{2,1,0:T(8,128)(2,1)} custom-call(s32[8]{0:T(128)S(1)} %dynamic-slice_bitcast_fusion.table_ref, bf16[192,2048]{1,0:T(8,128)(2,1)} %copy-done.4, bf16[192,2048]{1,0:T(8,128)(2,1)} %collective-permute-done.6.refs_1_, bf16[192,2048]{1,0:T(8,128)(2,1)} %copy-done.6, bf16[192,2048]{1,0:T(8,128)(2,1)} %copy-done.7, ...), custom_call_target="tpu_custom_call" | custom-call | flops 1 | bytes 1 | tf_op jit(solution)/shard_map/weight_grad/pallas_call | solution.py:492
  366.1 7.5 %collective-permute-done.23.refs_5_ = bf16[192,2048]{1,0:T(8,128)(2,1)S(1)} collective-permute-done((bf16[192,2048]{1,0:T(8,128)(2,1)}, bf16[192,2048]{1,0:T(8,128)(2,1)S(1)}, u32[]{:S(2)}, u32[]{:S(2)}) %collective-permute-start.23) | collective-permute-done | bytes 786464 | tf_op jit(solution)/shard_map/ppermute | solution.py:797
  388.5 6.5 %all-to-all-done.4 = bf16[4,320,128]{2,1,0:T(8,128)(2,1)S(1)} async-done(((bf16[4,320,128]{2,1,0:T(8,128)(2,1)}), bf16[4,320,128]{2,1,0:T(8,128)(2,1)S(1)}, u32[]{:S(2)}, u32[]{:S(2)}) %all-to-all-start.4) | async-done | bytes 327712 | tf_op jit(solution)/shard_map/all_to_all | solution.py:743
  415.2 8.0 %collective-permute-done.28 = bf16[48,2048]{1,0:T(8,128)(2,1)S(1)} collective-permute-done((bf16[48,2048]{1,0:T(8,128)(2,1)S(1)}, bf16[48,2048]{1,0:T(8,128)(2,1)S(1)}, u32[]{:S(2)}, u32[]{:S(2)}) %collective-permute-start.28) | collective-permute-done | bytes 196640 | tf_op jit(solution)/shard_map/ppermute | solution.py:734
  423.2 7.4 %collective-permute-done.27 = bf16[48,2048]{1,0:T(8,128)(2,1)S(1)} collective-permute-done((bf16[48,2048]{1,0:T(8,128)(2,1)S(1)}, bf16[48,2048]{1,0:T(8,128)(2,1)S(1)}, u32[]{:S(2)}, u32[]{:S(2)}) %collective-permute-start.27) | collective-permute-done | bytes 196640 | tf_op jit(solution)/shard_map/ppermute | solution.py:734
  432.5 6.1 %own_kernel.1 = (bf16[48,2048]{1,0:T(8,128)(2,1)}, bf16[48,2048]{1,0:T(8,128)(2,1)}, bf16[48,2048]{1,0:T(8,128)(2,1)}, bf16[48,2048]{1,0:T(8,128)(2,1)}) custom-call(s32[8]{0:T(128)S(1)} %dynamic-slice_bitcast_fusion.table_ref, bf16[1536,1024]{1,0:T(8,128)(2,1)} %get-tuple-element.191.g_ref.ga_ref.gb_ref.refs_8_.refs_9_.refs_10_.refs_11_.refs_12_.refs_13_.refs_14_.refs_15_, ...), custom_call_target="tpu_custom_call" | custom-call | flops 1 | bytes 1 | tf_op jit(solution)/shard_map/own_kernel/pallas_call | solution.py:643
  (289 shorter events, 162.9 us)
Async XLA Ops:
  7.2 71.0 %all-gather.6.cloned.1.call-start = ((), (), s32[]{:S(2)}) async-start(), calls=%async_computation.9 | async-start | bytes 5242880 | tf_op jit(solution)/shard_map/all_gather | solution.py:842
  32.1 174.2 %all-gather.10.cloned.1.call-start = ((), (), s32[]{:S(2)}) async-start(), calls=%async_computation.11 | async-start | bytes 2621440 | tf_op jit(solution)/shard_map/all_gather | solution.py:896
  32.5 19.8 %collective-permute-start.7 = (bf16[192,2048]{1,0:T(8,128)(2,1)S(1)}, bf16[192,2048]{1,0:T(8,128)(2,1)S(1)}, u32[]{:S(2)}, u32[]{:S(2)}) collective-permute-start(bf16[192,2048]{1,0:T(8,128)(2,1)S(1)} %convolution_convert_fusion.4.refs_0_), channel_id=1, source_target_pairs={{1,0},{3,1},{5,3},{7,5},{6,7},{4,6},{2,4},{0,2},{9,8},{11,9},{13,1... | collective-permute-start | bytes 2359304 | tf_op jit(solution)/shard_map/ppermute | solution.py:797
  34.1 19.5 %collective-permute-start.6 = (bf16[192,2048]{1,0:T(8,128)(2,1)S(1)}, bf16[192,2048]{1,0:T(8,128)(2,1)}, u32[]{:S(2)}, u32[]{:S(2)}) collective-permute-start(bf16[192,2048]{1,0:T(8,128)(2,1)S(1)} %convolution_convert_fusion.4.refs_0_), channel_id=1, source_target_pairs={{0,1},{1,3},{3,5},{5,7},{7,6},{6,4},{4,2},{2,0},{8,9},{9,11},{11,1... | collective-permute-start | bytes 2359304 | tf_op jit(solution)/shard_map/ppermute | solution.py:797
  53.7 18.8 %collective-permute-start.8 = (bf16[192,2048]{1,0:T(8,128)(2,1)}, bf16[192,2048]{1,0:T(8,128)(2,1)S(1)}, u32[]{:S(2)}, u32[]{:S(2)}) collective-permute-start(bf16[192,2048]{1,0:T(8,128)(2,1)} %collective-permute-done.6.refs_1_), channel_id=1, source_target_pairs={{0,1},{1,3},{3,5},{5,7},{7,6},{6,4},{4,2},{2,0},{8,9},{9,11},{11,1... | collective-permute-start | bytes 2359304 | tf_op jit(solution)/shard_map/ppermute | solution.py:797
  54.1 18.4 %collective-permute-start.9 = (bf16[192,2048]{1,0:T(8,128)(2,1)S(1)}, bf16[192,2048]{1,0:T(8,128)(2,1)S(1)}, u32[]{:S(2)}, u32[]{:S(2)}) collective-permute-start(bf16[192,2048]{1,0:T(8,128)(2,1)S(1)} %collective-permute-done.7.refs_2_), channel_id=1, source_target_pairs={{1,0},{3,1},{5,3},{7,5},{6,7},{4,6},{2,4},{0,2},{9,8},{11,9},{13,1... | collective-permute-start | bytes 2359304 | tf_op jit(solution)/shard_map/ppermute | solution.py:797
  73.5 144.8 %all-gather.8.cloned.1.call-start = ((), (), s32[]{:S(2)}) async-start(), calls=%async_computation.10 | async-start | bytes 7077888 | tf_op jit(solution)/shard_map/all_gather | solution.py:897
  75.6 20.2 %collective-permute-start.17 = (bf16[48,2048]{1,0:T(8,128)(2,1)S(1)}, bf16[48,2048]{1,0:T(8,128)(2,1)S(1)}, u32[]{:S(2)}, u32[]{:S(2)}) collective-permute-start(bf16[48,2048]{1,0:T(8,128)(2,1)S(1)} %get-tuple-element.140), channel_id=1, source_target_pairs={{0,8},{8,0},{16,24},{24,16},{1,9},{9,1},{17,25},{25,17},{2,10},{10... | collective-permute-start | bytes 589832 | tf_op jit(solution)/shard_map/ppermute | solution.py:734
  75.7 20.2 %collective-permute-start.18 = (bf16[48,2048]{1,0:T(8,128)(2,1)S(1)}, bf16[48,2048]{1,0:T(8,128)(2,1)}, u32[]{:S(2)}, u32[]{:S(2)}) collective-permute-start(bf16[48,2048]{1,0:T(8,128)(2,1)S(1)} %get-tuple-element.141), channel_id=1, source_target_pairs={{0,16},{8,24},{16,0},{24,8},{1,17},{9,25},{17,1},{25,9},{2,18},{10... | collective-permute-start | bytes 589832 | tf_op jit(solution)/shard_map/ppermute | solution.py:734
  76.3 19.6 %collective-permute-start.19 = (bf16[48,2048]{1,0:T(8,128)(2,1)S(1)}, bf16[48,2048]{1,0:T(8,128)(2,1)}, u32[]{:S(2)}, u32[]{:S(2)}) collective-permute-start(bf16[48,2048]{1,0:T(8,128)(2,1)S(1)} %get-tuple-element.142), channel_id=1, source_target_pairs={{0,24},{8,16},{16,8},{24,0},{1,25},{9,17},{17,9},{25,1},{2,26},{10... | collective-permute-start | bytes 589832 | tf_op jit(solution)/shard_map/ppermute | solution.py:734
  119.1 31.8 %all-to-all-start = ((bf16[8,240,128]{2,1,0:T(8,128)(2,1)}), bf16[8,240,128]{2,1,0:T(8,128)(2,1)S(1)}, u32[]{:S(2)}, u32[]{:S(2)}) async-start(bf16[8,240,128]{2,1,0:T(8,128)(2,1)} %get-tuple-element.148), calls=%async_computation | async-start | bytes 983040 | tf_op jit(solution)/shard_map/all_to_all | solution.py:743
  151.8 29.0 %all-to-all-start.1 = ((bf16[8,240,128]{2,1,0:T(8,128)(2,1)}), bf16[8,240,128]{2,1,0:T(8,128)(2,1)S(1)}, u32[]{:S(2)}, u32[]{:S(2)}) async-start(bf16[8,240,128]{2,1,0:T(8,128)(2,1)} %broadcast_in_dim.26), calls=%async_computation.1 | async-start | bytes 983040 | tf_op jit(solution)/shard_map/all_to_all | solution.py:743
  155.3 193.1 %reduce-scatter.4.cloned.1.call-start = ((), (), s32[]{:S(2)}) async-start(), calls=%async_computation.12 | async-start | bytes 7077888 | tf_op jit(solution)/shard_map/reduce_scatter | solution.py:917
  279.0 17.8 %all-to-all-start.2 = ((bf16[8,240,128]{2,1,0:T(8,128)(2,1)}), bf16[8,240,128]{2,1,0:T(8,128)(2,1)S(1)}, u32[]{:S(2)}, u32[]{:S(2)}) async-start(bf16[8,240,128]{2,1,0:T(8,128)(2,1)} %get-tuple-element.162), calls=%async_computation.2 | async-start | bytes 983040 | tf_op jit(solution)/shard_map/all_to_all | solution.py:743
  298.1 25.9 %all-to-all-start.3 = ((bf16[8,240,128]{2,1,0:T(8,128)(2,1)}), bf16[8,240,128]{2,1,0:T(8,128)(2,1)S(1)}, u32[]{:S(2)}, u32[]{:S(2)}) async-start(bf16[8,240,128]{2,1,0:T(8,128)(2,1)} %broadcast_in_dim.29), calls=%async_computation.3 | async-start | bytes 983040 | tf_op jit(solution)/shard_map/all_to_all | solution.py:743
  301.7 97.9 %reduce-scatter.6.cloned.1.call-start = ((), (), s32[]{:S(2)}) async-start(), calls=%async_computation.13 | async-start | bytes 5242880 | tf_op jit(solution)/shard_map/reduce_scatter | solution.py:953
  324.0 114.6 %reduce-scatter.8.cloned.1.call-start = ((), (), s32[]{:S(2)}) async-start(), calls=%async_computation.14 | async-start | bytes 2621440 | tf_op jit(solution)/shard_map/reduce_scatter | solution.py:979
  354.1 19.5 %collective-permute-start.23 = (bf16[192,2048]{1,0:T(8,128)(2,1)}, bf16[192,2048]{1,0:T(8,128)(2,1)S(1)}, u32[]{:S(2)}, u32[]{:S(2)}) collective-permute-start(bf16[192,2048]{1,0:T(8,128)(2,1)} %get-tuple-element.189), channel_id=1, source_target_pairs={{1,0},{3,1},{5,3},{7,5},{6,7},{4,6},{2,4},{0,2},{9,8},{11,9},{13,1... | collective-permute-start | bytes 2359304 | tf_op jit(solution)/shard_map/ppermute | solution.py:797
  355.9 19.2 %collective-permute-start.22 = (bf16[192,2048]{1,0:T(8,128)(2,1)}, bf16[192,2048]{1,0:T(8,128)(2,1)S(1)}, u32[]{:S(2)}, u32[]{:S(2)}) collective-permute-start(bf16[192,2048]{1,0:T(8,128)(2,1)} %get-tuple-element.188), channel_id=1, source_target_pairs={{0,1},{1,3},{3,5},{5,7},{7,6},{6,4},{4,2},{2,0},{8,9},{9,11},{11,1... | collective-permute-start | bytes 2359304 | tf_op jit(solution)/shard_map/ppermute | solution.py:797
  381.0 18.7 %collective-permute-start.24 = (bf16[192,2048]{1,0:T(8,128)(2,1)}, bf16[192,2048]{1,0:T(8,128)(2,1)}, u32[]{:S(2)}, u32[]{:S(2)}) collective-permute-start(bf16[192,2048]{1,0:T(8,128)(2,1)} %get-tuple-element.199), channel_id=1, source_target_pairs={{0,1},{1,3},{3,5},{5,7},{7,6},{6,4},{4,2},{2,0},{8,9},{9,11},{11,1... | collective-permute-start | bytes 2359304 | tf_op jit(solution)/shard_map/ppermute | solution.py:797
  381.7 18.0 %collective-permute-start.25 = (bf16[192,2048]{1,0:T(8,128)(2,1)}, bf16[192,2048]{1,0:T(8,128)(2,1)}, u32[]{:S(2)}, u32[]{:S(2)}) collective-permute-start(bf16[192,2048]{1,0:T(8,128)(2,1)} %get-tuple-element.200), channel_id=1, source_target_pairs={{1,0},{3,1},{5,3},{7,5},{6,7},{4,6},{2,4},{0,2},{9,8},{11,9},{13,1... | collective-permute-start | bytes 2359304 | tf_op jit(solution)/shard_map/ppermute | solution.py:797
  409.5 21.3 %collective-permute-start.29 = (bf16[192,2048]{1,0:T(8,128)(2,1)}, bf16[192,2048]{1,0:T(8,128)(2,1)S(1)}, u32[]{:S(2)}, u32[]{:S(2)}) collective-permute-start(bf16[192,2048]{1,0:T(8,128)(2,1)} %get-tuple-element.214), channel_id=1, source_target_pairs={{0,1},{1,3},{3,5},{5,7},{7,6},{6,4},{4,2},{2,0},{8,9},{9,11},{11,1... | collective-permute-start | bytes 2359304 | tf_op jit(solution)/shard_map/ppermute | solution.py:797
  410.8 20.0 %collective-permute-start.30 = (bf16[192,2048]{1,0:T(8,128)(2,1)}, bf16[192,2048]{1,0:T(8,128)(2,1)S(1)}, u32[]{:S(2)}, u32[]{:S(2)}) collective-permute-start(bf16[192,2048]{1,0:T(8,128)(2,1)} %get-tuple-element.215), channel_id=1, source_target_pairs={{1,0},{3,1},{5,3},{7,5},{6,7},{4,6},{2,4},{0,2},{9,8},{11,9},{13,1... | collective-permute-start | bytes 2359304 | tf_op jit(solution)/shard_map/ppermute | solution.py:797
  412.0 18.6 %collective-permute-start.27 = (bf16[48,2048]{1,0:T(8,128)(2,1)S(1)}, bf16[48,2048]{1,0:T(8,128)(2,1)S(1)}, u32[]{:S(2)}, u32[]{:S(2)}) collective-permute-start(bf16[48,2048]{1,0:T(8,128)(2,1)S(1)} %get-tuple-element.235), channel_id=1, source_target_pairs={{0,16},{8,24},{16,0},{24,8},{1,17},{9,25},{17,1},{25,9},{2,18},{10... | collective-permute-start | bytes 589832 | tf_op jit(solution)/shard_map/ppermute | solution.py:734
  (61 other events, 476.7 us)
Sparse Core Ops, SparseCore 0:
  32.2 37.6 all-gather.5
  73.6 26.2 all-gather.9
  105.4 112.8 all-gather.7
  221.8 122.1 reduce-scatter.3
  346.3 42.4 reduce-scatter.5
  391.9 38.6 reduce-scatter.7

commit v3 on v2

--- a/solution.py
+++ b/solution.py
@@ -962,11 +962,11 @@
         names = []
         if k == 0:
             bag["grads"] = grad_projected
-            names = ["mixed", "sums", "grads"]
+            names = ["sums", "grads"]
         if k == 1:
             bag["inner"] = weight_grad(
                 ring.at, distances, normed_shards, after(bag["grads"], sent), 0, channels, dp_size, False)
-            names = ["mixed", "sums", "inner"]
+            names = ["sums", "inner"]
         if k == half - 2:
             flat, more = pack_conv(*after(tuple(bag["sums"]), sent))
             sizes.extend(more)

time: 478 us -> 478 us (level)
  no operation moved by 1% of the time
where the time goes in v3:
time: 478 us; the launch traced here: 468 us
  Pallas kernels  174 us (36%)
  waiting for transfers between devices  156 us (33%)
  starting transfers between devices  54.9 us (11%)
  matrix products  28.8 us (6%)
  local copies, waits for them, and re-layouts  19.4 us (4%)
  between operations  15.4 us (3%)
  other arithmetic  14.5 us (3%)
  blocking collectives  5.52 us (1%)
    all_to_all x6, waiting for transfers between devices, swap(): return lax.all_to_all(values, axis, split_axis=0, concat_axis=0, tiled=True)  64.9 us
    pallas_call x1, Pallas kernels, scan_backward(): pl.pallas_call(functools.partial(backward_kernel, len(whole)), name='scan...  52.1 us
    ppermute x16, waiting for transfers between devices, hop(): lax.ppermute(value, self.axis, self.forward if ahead else self.backward)  50.5 us
    ppermute x18, waiting for transfers between devices, flip(): lax.ppermute(value, axis, [(i, i ^ bit) for i in range(lax.axis_size(axis...  37.1 us
    dot_general x8, matrix products, mm(): return lax.dot_general(a, b, dims, preferred_element_type=F32)  28.8 us
    pallas_call x3, Pallas kernels, weight_grad(): pl.pallas_call(functools.partial(weight_grad_kernel, count, turned), name...  26.2 us
    pallas_call x1, Pallas kernels, scan_forward(): pl.pallas_call(functools.partial(forward_kernel, len(whole)), name='scan_...  25.4 us
    pallas_call x5, Pallas kernels, ring_step(): pl.pallas_call(functools.partial(kernel, cuts, halves=True) if small else...  25.1 us
  transfers between devices with their start and end apart: 46, of which 28 were waited for; matrix products, arithmetic and copies ran while one was open for 10% of the time, Pallas kernels for 37%

profile of v3, /device:TPU:0, one launch (start us, length us, event | category | flops | bytes accessed | tf_op | source)
XLA Modules:
  0.0 468.5 jit_solution(3155780005017450779)
XLA Ops:
  34.8 17.4 %collective-permute-done.7.refs_2_ = bf16[192,2048]{1,0:T(8,128)(2,1)S(1)} collective-permute-done((bf16[192,2048]{1,0:T(8,128)(2,1)S(1)}, bf16[192,2048]{1,0:T(8,128)(2,1)S(1)}, u32[]{:S(2)}, u32[]{:S(2)}) %collective-permute-start.7) | collective-permute-done | bytes 786464 | tf_op jit(solution)/shard_map/ppermute | solution.py:797
  64.0 8.5 %collective-permute-done.8.refs_3_ = bf16[192,2048]{1,0:T(8,128)(2,1)S(1)} collective-permute-done((bf16[192,2048]{1,0:T(8,128)(2,1)}, bf16[192,2048]{1,0:T(8,128)(2,1)S(1)}, u32[]{:S(2)}, u32[]{:S(2)}) %collective-permute-start.8) | collective-permute-done | bytes 786464 | tf_op jit(solution)/shard_map/ppermute | solution.py:797
  78.2 11.8 %placed_product.2.refs_3_ = bf16[1536,1024]{1,0:T(8,128)(2,1)} custom-call(s32[8]{0:T(128)S(1)} %dynamic-slice_bitcast_fusion.table_ref, bf16[192,2048]{1,0:T(8,128)(2,1)} %copy-done.4, bf16[192,2048]{1,0:T(8,128)(2,1)} %collective-permute-done.6.refs_1_, bf16[192,2048]{1,0:T(8,128)(2,1)} %copy-done.6, ...), custom_call_target="tpu_custom_call", output_to_operand_aliasing={{}: (7, {})} | custom-call | flops 1 | bytes 1 | tf_op jit(solution)/shard_map/placed_product/pallas_call | solution.py:537
  97.0 6.8 %placed_product.3.refs_8_ = bf16[1536,1024]{1,0:T(8,128)(2,1)} custom-call(s32[8]{0:T(128)S(1)} %dynamic-slice_bitcast_fusion.table_ref, bf16[192,2048]{1,0:T(8,128)(2,1)} %copy-done.5, bf16[192,2048]{1,0:T(8,128)(2,1)} %collective-permute-done.14.refs_1_.refs_6_, ...), custom_call_target="tpu_custom_call", output_to_operand_aliasing={{}: (4, {})} | custom-call | flops 1 | bytes 1 | tf_op jit(solution)/shard_map/placed_product/pallas_call | solution.py:537
  111.3 7.9 %front.1 = (bf16[1536,512]{1,0:T(8,128)(2,1)}, bf16[8,240,128]{2,1,0:T(8,128)(2,1)}) custom-call(s32[1]{0:T(128)} %constant.78.clone.1.me_ref, bf16[1536,1024]{1,0:T(8,128)(2,1)} %placed_halves.1.inner_ref.gate_ref.prior_ref, s32[1536,1]{1,0:T(8,128)S(1)} %reshape_subtract_fusion.offset_ref, f32[4,512]{1,0:T(4,128)S(1)} %slice.188.taps_ref, ...), custom_call_target="tpu_custom_call" | custom-call | flops 1 | bytes 1 | tf_op jit(solution)/shard_map/front/pallas_call | solution.py:87
  123.9 5.5 %all-gather.1 = bf16[4,36,512]{2,1,0:T(8,128)(2,1)S(1)} all-gather(bf16[1,36,512]{2,1,0:T(8,128)(2,1)S(1)} %bitcast.155), channel_id=2, replica_groups=mesh['dp'=4,'tensor'=8] {'dp'}, dimensions={0}, use_global_device_ids=true | all-gather | bytes 184320 | tf_op jit(solution)/shard_map/all_gather | solution.py:898
  131.4 19.5 %all-to-all-done = bf16[8,240,128]{2,1,0:T(8,128)(2,1)S(1)} async-done(((bf16[8,240,128]{2,1,0:T(8,128)(2,1)}), bf16[8,240,128]{2,1,0:T(8,128)(2,1)S(1)}, u32[]{:S(2)}, u32[]{:S(2)}) %all-to-all-start) | async-done | bytes 491552 | tf_op jit(solution)/shard_map/all_to_all | solution.py:743
  155.7 25.2 %all-to-all-done.1.pack_ref = bf16[8,240,128]{2,1,0:T(8,128)(2,1)S(1)} async-done(((bf16[8,240,128]{2,1,0:T(8,128)(2,1)}), bf16[8,240,128]{2,1,0:T(8,128)(2,1)S(1)}, u32[]{:S(2)}, u32[]{:S(2)}) %all-to-all-start.1) | async-done | bytes 491552 | tf_op jit(solution)/shard_map/all_to_all | solution.py:743
  180.8 25.4 %scan_forward.1 = (f32[1536,512]{1,0:T(8,128)}, f32[1536,512]{1,0:T(8,128)}, f32[1536,512]{1,0:T(8,128)}, bf16[1536,512]{1,0:T(8,128)(2,1)}, bf16[24576,512]{1,0:T(8,128)(2,1)}, /*index=5*/f32[16,512]{1,0:T(8,128)}) custom-call(s32[1]{0:T(128)} %constant.78.clone.1.me_ref, bf16[8,240,128]{2,1,0:T(8,128)(2,1)S(1)} %all-to-all-done.1.pack_ref, ...), custom_call_target="tpu_custom_call" | custom-call | flops 1 | bytes 1 | tf_op jit(solution)/shard_map/scan_forward/pallas_call | solution.py:185
  206.3 8.2 %convolution_convert_fusion = bf16[1536,2048]{1,0:T(8,128)(2,1)} fusion(bf16[1536,512]{1,0:T(8,128)(2,1)} %get-tuple-element.162.refs_1_, bf16[512,2048]{1,0:T(8,128)(2,1)} %all-gather.10.cloned.1.call-done), kind=kOutput, calls=%fused_computation | convolution fusion | flops 3224371200 | bytes 9961472 | tf_op jit(solution)/shard_map/dot_general | solution.py:31
  218.3 8.5 %fusion.25.gg_ref = f32[1536,512]{1,0:T(8,128)} fusion(bf16[1536,2048]{1,0:T(8,128)(2,1)} %all-gather.8.cloned.1.call-done.refs_0_, bf16[512,2048]{1,0:T(8,128)(2,1)} %all-gather.10.cloned.1.call-done), kind=kOutput, calls=%fused_computation.91 | convolution fusion | flops 3221225472 | bytes 11534336 | tf_op jit(solution)/shard_map/dot_general | solution.py:31
  226.9 52.1 %scan_backward.1 = (bf16[1536,1024]{1,0:T(8,128)(2,1)}, f32[1536,512]{1,0:T(8,128)}, bf16[8,240,128]{2,1,0:T(8,128)(2,1)}, f32[16,512]{1,0:T(8,128)}, f32[16,512...) custom-call(s32[1]{0:T(128)} %constant.78.clone.1.me_ref, ...), custom_call_target="tpu_custom_call" | custom-call | flops 1 | bytes 1 | tf_op jit(solution)/shard_map/scan_backward/pallas_call | solution.py:343
  283.0 8.5 %weight_grad.3.refs_16_ = bf16[4,1024,512]{2,1,0:T(8,128)(2,1)} custom-call(s32[8]{0:T(128)S(1)} %dynamic-slice_bitcast_fusion.table_ref, bf16[1536,2048]{1,0:T(8,128)(2,1)} %all-gather.8.cloned.1.call-done.refs_0_, bf16[1536,512]{1,0:T(8,128)(2,1)} %get-tuple-element.162.refs_1_), custom_call_target="tpu_custom_call" | custom-call | flops 1 | bytes 1 | tf_op jit(solution)/shard_map/weight_grad/pallas_call | solution.py:492
  291.4 5.4 %all-to-all-done.2 = bf16[8,240,128]{2,1,0:T(8,128)(2,1)S(1)} async-done(((bf16[8,240,128]{2,1,0:T(8,128)(2,1)}), bf16[8,240,128]{2,1,0:T(8,128)(2,1)S(1)}, u32[]{:S(2)}, u32[]{:S(2)}) %all-to-all-start.2) | async-done | bytes 491552 | tf_op jit(solution)/shard_map/all_to_all | solution.py:743
  301.9 8.7 %weight_grad.4 = bf16[4,1024,512]{2,1,0:T(8,128)(2,1)} custom-call(s32[8]{0:T(128)S(1)} %dynamic-slice_bitcast_fusion.table_ref, bf16[192,2048]{1,0:T(8,128)(2,1)} %copy-done.4, bf16[192,2048]{1,0:T(8,128)(2,1)} %collective-permute-done.6.refs_1_, bf16[192,2048]{1,0:T(8,128)(2,1)} %copy-done.6, ...), custom_call_target="tpu_custom_call", output_to_operand_aliasing={{}: (17, {})} | custom-call | flops 1 | bytes 1 | tf_op jit(solution)/shard_map/weight_grad/pallas_call | solution.py:492
  310.6 8.2 %convolution_convert_fusion.1.t_ref.ta_ref.tb_ref = bf16[1536,2048]{1,0:T(8,128)(2,1)} fusion(bf16[2048,1024]{1,0:T(8,128)(2,1)} %all-gather.6.cloned.1.call-done.refs_5_.refs_2_.refs_0_.refs_1_.refs_3_.refs_4_.refs_6_.refs_7_, bf16[1536,1024]{1,0:T(8,128)(2,1)} %get-tuple-element.166.refs_8_.refs_9_.refs_10_.refs_11_.refs_12_.refs_13_.refs_14_.refs_15_.grad_ref), kind=kOutput, calls=%fused_computation.1 | convolution fusion | flops 3224371200 | bytes 9961472 | tf_op jit(solution)/shard_map/dot_general | solution.py:31
  324.1 11.3 %end.1 = (bf16[1536,1024]{1,0:T(8,128)(2,1)}, f32[8,512]{1,0:T(8,128)S(1)}, f32[512,128]{1,0:T(8,128)S(1)}, f32[32,512]{1,0:T(8,128)S(1)}) custom-call(s32[1]{0:T(128)} %constant.78.clone.1.me_ref, bf16[8,240,128]{2,1,0:T(8,128)(2,1)S(1)} %all-to-all-done.3.pack_ref, f32[1536,512]{1,0:T(8,128)} %get-tuple-element.175.gact_ref, ...), custom_call_target="tpu_custom_call", output_to_operand_aliasing={{0}: (11, {})} | custom-call | flops 1 | bytes 1 | tf_op jit(solution)/shard_map/end/pallas_call | solution.py:424
  341.7 6.7 %collective-permute-done.20.refs_4_ = bf16[192,1024]{1,0:T(8,128)(2,1)S(1)} collective-permute-done((bf16[192,1024]{1,0:T(8,128)(2,1)}, bf16[192,1024]{1,0:T(8,128)(2,1)S(1)}, u32[]{:S(2)}, u32[]{:S(2)}) %collective-permute-start.20) | collective-permute-done | bytes 393248 | tf_op jit(solution)/shard_map/ppermute | solution.py:797
  357.2 9.0 %weight_grad.5 = bf16[4,512,512]{2,1,0:T(8,128)(2,1)} custom-call(s32[8]{0:T(128)S(1)} %dynamic-slice_bitcast_fusion.table_ref, bf16[192,2048]{1,0:T(8,128)(2,1)} %copy-done.4, bf16[192,2048]{1,0:T(8,128)(2,1)} %collective-permute-done.6.refs_1_, bf16[192,2048]{1,0:T(8,128)(2,1)} %copy-done.6, bf16[192,2048]{1,0:T(8,128)(2,1)} %copy-done.7, ...), custom_call_target="tpu_custom_call" | custom-call | flops 1 | bytes 1 | tf_op jit(solution)/shard_map/weight_grad/pallas_call | solution.py:492
  366.2 7.4 %collective-permute-done.23.refs_5_ = bf16[192,2048]{1,0:T(8,128)(2,1)S(1)} collective-permute-done((bf16[192,2048]{1,0:T(8,128)(2,1)}, bf16[192,2048]{1,0:T(8,128)(2,1)S(1)}, u32[]{:S(2)}, u32[]{:S(2)}) %collective-permute-start.23) | collective-permute-done | bytes 786464 | tf_op jit(solution)/shard_map/ppermute | solution.py:797
  388.5 6.5 %all-to-all-done.4 = bf16[4,320,128]{2,1,0:T(8,128)(2,1)S(1)} async-done(((bf16[4,320,128]{2,1,0:T(8,128)(2,1)}), bf16[4,320,128]{2,1,0:T(8,128)(2,1)S(1)}, u32[]{:S(2)}, u32[]{:S(2)}) %all-to-all-start.4) | async-done | bytes 327712 | tf_op jit(solution)/shard_map/all_to_all | solution.py:743
  415.2 8.0 %collective-permute-done.28 = bf16[48,2048]{1,0:T(8,128)(2,1)S(1)} collective-permute-done((bf16[48,2048]{1,0:T(8,128)(2,1)S(1)}, bf16[48,2048]{1,0:T(8,128)(2,1)S(1)}, u32[]{:S(2)}, u32[]{:S(2)}) %collective-permute-start.28) | collective-permute-done | bytes 196640 | tf_op jit(solution)/shard_map/ppermute | solution.py:734
  423.3 7.4 %collective-permute-done.27 = bf16[48,2048]{1,0:T(8,128)(2,1)S(1)} collective-permute-done((bf16[48,2048]{1,0:T(8,128)(2,1)S(1)}, bf16[48,2048]{1,0:T(8,128)(2,1)S(1)}, u32[]{:S(2)}, u32[]{:S(2)}) %collective-permute-start.27) | collective-permute-done | bytes 196640 | tf_op jit(solution)/shard_map/ppermute | solution.py:734
  432.5 6.1 %own_kernel.1 = (bf16[48,2048]{1,0:T(8,128)(2,1)}, bf16[48,2048]{1,0:T(8,128)(2,1)}, bf16[48,2048]{1,0:T(8,128)(2,1)}, bf16[48,2048]{1,0:T(8,128)(2,1)}) custom-call(s32[8]{0:T(128)S(1)} %dynamic-slice_bitcast_fusion.table_ref, bf16[1536,1024]{1,0:T(8,128)(2,1)} %get-tuple-element.189.g_ref.ga_ref.gb_ref.refs_8_.refs_9_.refs_10_.refs_11_.refs_12_.refs_13_.refs_14_.refs_15_, ...), custom_call_target="tpu_custom_call" | custom-call | flops 1 | bytes 1 | tf_op jit(solution)/shard_map/own_kernel/pallas_call | solution.py:643
  (289 shorter events, 162.9 us)
Async XLA Ops:
  7.2 71.0 %all-gather.6.cloned.1.call-start = ((), (), s32[]{:S(2)}) async-start(), calls=%async_computation.9 | async-start | bytes 5242880 | tf_op jit(solution)/shard_map/all_gather | solution.py:842
  32.1 174.2 %all-gather.10.cloned.1.call-start = ((), (), s32[]{:S(2)}) async-start(), calls=%async_computation.11 | async-start | bytes 2621440 | tf_op jit(solution)/shard_map/all_gather | solution.py:896
  32.5 19.8 %collective-permute-start.7 = (bf16[192,2048]{1,0:T(8,128)(2,1)S(1)}, bf16[192,2048]{1,0:T(8,128)(2,1)S(1)}, u32[]{:S(2)}, u32[]{:S(2)}) collective-permute-start(bf16[192,2048]{1,0:T(8,128)(2,1)S(1)} %convolution_convert_fusion.4.refs_0_), channel_id=1, source_target_pairs={{1,0},{3,1},{5,3},{7,5},{6,7},{4,6},{2,4},{0,2},{9,8},{11,9},{13,1... | collective-permute-start | bytes 2359304 | tf_op jit(solution)/shard_map/ppermute | solution.py:797
  34.1 19.5 %collective-permute-start.6 = (bf16[192,2048]{1,0:T(8,128)(2,1)S(1)}, bf16[192,2048]{1,0:T(8,128)(2,1)}, u32[]{:S(2)}, u32[]{:S(2)}) collective-permute-start(bf16[192,2048]{1,0:T(8,128)(2,1)S(1)} %convolution_convert_fusion.4.refs_0_), channel_id=1, source_target_pairs={{0,1},{1,3},{3,5},{5,7},{7,6},{6,4},{4,2},{2,0},{8,9},{9,11},{11,1... | collective-permute-start | bytes 2359304 | tf_op jit(solution)/shard_map/ppermute | solution.py:797
  53.7 18.8 %collective-permute-start.8 = (bf16[192,2048]{1,0:T(8,128)(2,1)}, bf16[192,2048]{1,0:T(8,128)(2,1)S(1)}, u32[]{:S(2)}, u32[]{:S(2)}) collective-permute-start(bf16[192,2048]{1,0:T(8,128)(2,1)} %collective-permute-done.6.refs_1_), channel_id=1, source_target_pairs={{0,1},{1,3},{3,5},{5,7},{7,6},{6,4},{4,2},{2,0},{8,9},{9,11},{11,1... | collective-permute-start | bytes 2359304 | tf_op jit(solution)/shard_map/ppermute | solution.py:797
  54.1 18.4 %collective-permute-start.9 = (bf16[192,2048]{1,0:T(8,128)(2,1)S(1)}, bf16[192,2048]{1,0:T(8,128)(2,1)S(1)}, u32[]{:S(2)}, u32[]{:S(2)}) collective-permute-start(bf16[192,2048]{1,0:T(8,128)(2,1)S(1)} %collective-permute-done.7.refs_2_), channel_id=1, source_target_pairs={{1,0},{3,1},{5,3},{7,5},{6,7},{4,6},{2,4},{0,2},{9,8},{11,9},{13,1... | collective-permute-start | bytes 2359304 | tf_op jit(solution)/shard_map/ppermute | solution.py:797
  73.5 144.8 %all-gather.8.cloned.1.call-start = ((), (), s32[]{:S(2)}) async-start(), calls=%async_computation.10 | async-start | bytes 7077888 | tf_op jit(solution)/shard_map/all_gather | solution.py:897
  75.6 20.2 %collective-permute-start.17 = (bf16[48,2048]{1,0:T(8,128)(2,1)S(1)}, bf16[48,2048]{1,0:T(8,128)(2,1)S(1)}, u32[]{:S(2)}, u32[]{:S(2)}) collective-permute-start(bf16[48,2048]{1,0:T(8,128)(2,1)S(1)} %get-tuple-element.138), channel_id=1, source_target_pairs={{0,8},{8,0},{16,24},{24,16},{1,9},{9,1},{17,25},{25,17},{2,10},{10... | collective-permute-start | bytes 589832 | tf_op jit(solution)/shard_map/ppermute | solution.py:734
  75.7 20.2 %collective-permute-start.18 = (bf16[48,2048]{1,0:T(8,128)(2,1)S(1)}, bf16[48,2048]{1,0:T(8,128)(2,1)}, u32[]{:S(2)}, u32[]{:S(2)}) collective-permute-start(bf16[48,2048]{1,0:T(8,128)(2,1)S(1)} %get-tuple-element.139), channel_id=1, source_target_pairs={{0,16},{8,24},{16,0},{24,8},{1,17},{9,25},{17,1},{25,9},{2,18},{10... | collective-permute-start | bytes 589832 | tf_op jit(solution)/shard_map/ppermute | solution.py:734
  76.3 19.6 %collective-permute-start.19 = (bf16[48,2048]{1,0:T(8,128)(2,1)S(1)}, bf16[48,2048]{1,0:T(8,128)(2,1)}, u32[]{:S(2)}, u32[]{:S(2)}) collective-permute-start(bf16[48,2048]{1,0:T(8,128)(2,1)S(1)} %get-tuple-element.140), channel_id=1, source_target_pairs={{0,24},{8,16},{16,8},{24,0},{1,25},{9,17},{17,9},{25,1},{2,26},{10... | collective-permute-start | bytes 589832 | tf_op jit(solution)/shard_map/ppermute | solution.py:734
  119.2 31.8 %all-to-all-start = ((bf16[8,240,128]{2,1,0:T(8,128)(2,1)}), bf16[8,240,128]{2,1,0:T(8,128)(2,1)S(1)}, u32[]{:S(2)}, u32[]{:S(2)}) async-start(bf16[8,240,128]{2,1,0:T(8,128)(2,1)} %get-tuple-element.146), calls=%async_computation | async-start | bytes 983040 | tf_op jit(solution)/shard_map/all_to_all | solution.py:743
  151.9 29.0 %all-to-all-start.1 = ((bf16[8,240,128]{2,1,0:T(8,128)(2,1)}), bf16[8,240,128]{2,1,0:T(8,128)(2,1)S(1)}, u32[]{:S(2)}, u32[]{:S(2)}) async-start(bf16[8,240,128]{2,1,0:T(8,128)(2,1)} %broadcast_in_dim.26), calls=%async_computation.1 | async-start | bytes 983040 | tf_op jit(solution)/shard_map/all_to_all | solution.py:743
  155.4 239.7 %reduce-scatter.6.cloned.1.call-start = ((), (), s32[]{:S(2)}) async-start(), calls=%async_computation.13 | async-start | bytes 7077888 | tf_op jit(solution)/shard_map/reduce_scatter | solution.py:917
  279.0 17.8 %all-to-all-start.2 = ((bf16[8,240,128]{2,1,0:T(8,128)(2,1)}), bf16[8,240,128]{2,1,0:T(8,128)(2,1)S(1)}, u32[]{:S(2)}, u32[]{:S(2)}) async-start(bf16[8,240,128]{2,1,0:T(8,128)(2,1)} %get-tuple-element.160), calls=%async_computation.2 | async-start | bytes 983040 | tf_op jit(solution)/shard_map/all_to_all | solution.py:743
  298.1 25.9 %all-to-all-start.3 = ((bf16[8,240,128]{2,1,0:T(8,128)(2,1)}), bf16[8,240,128]{2,1,0:T(8,128)(2,1)S(1)}, u32[]{:S(2)}, u32[]{:S(2)}) async-start(bf16[8,240,128]{2,1,0:T(8,128)(2,1)} %broadcast_in_dim.29), calls=%async_computation.3 | async-start | bytes 983040 | tf_op jit(solution)/shard_map/all_to_all | solution.py:743
  301.7 98.0 %reduce-scatter.4.cloned.1.call-start = ((), (), s32[]{:S(2)}) async-start(), calls=%async_computation.12 | async-start | bytes 5242880 | tf_op jit(solution)/shard_map/reduce_scatter | solution.py:953
  324.0 114.6 %reduce-scatter.8.cloned.1.call-start = ((), (), s32[]{:S(2)}) async-start(), calls=%async_computation.14 | async-start | bytes 2621440 | tf_op jit(solution)/shard_map/reduce_scatter | solution.py:979
  354.1 19.5 %collective-permute-start.23 = (bf16[192,2048]{1,0:T(8,128)(2,1)}, bf16[192,2048]{1,0:T(8,128)(2,1)S(1)}, u32[]{:S(2)}, u32[]{:S(2)}) collective-permute-start(bf16[192,2048]{1,0:T(8,128)(2,1)} %get-tuple-element.187), channel_id=1, source_target_pairs={{1,0},{3,1},{5,3},{7,5},{6,7},{4,6},{2,4},{0,2},{9,8},{11,9},{13,1... | collective-permute-start | bytes 2359304 | tf_op jit(solution)/shard_map/ppermute | solution.py:797
  355.9 19.1 %collective-permute-start.22 = (bf16[192,2048]{1,0:T(8,128)(2,1)}, bf16[192,2048]{1,0:T(8,128)(2,1)S(1)}, u32[]{:S(2)}, u32[]{:S(2)}) collective-permute-start(bf16[192,2048]{1,0:T(8,128)(2,1)} %get-tuple-element.186), channel_id=1, source_target_pairs={{0,1},{1,3},{3,5},{5,7},{7,6},{6,4},{4,2},{2,0},{8,9},{9,11},{11,1... | collective-permute-start | bytes 2359304 | tf_op jit(solution)/shard_map/ppermute | solution.py:797
  381.0 18.7 %collective-permute-start.24 = (bf16[192,2048]{1,0:T(8,128)(2,1)}, bf16[192,2048]{1,0:T(8,128)(2,1)}, u32[]{:S(2)}, u32[]{:S(2)}) collective-permute-start(bf16[192,2048]{1,0:T(8,128)(2,1)} %get-tuple-element.196), channel_id=1, source_target_pairs={{0,1},{1,3},{3,5},{5,7},{7,6},{6,4},{4,2},{2,0},{8,9},{9,11},{11,1... | collective-permute-start | bytes 2359304 | tf_op jit(solution)/shard_map/ppermute | solution.py:797
  381.8 17.9 %collective-permute-start.25 = (bf16[192,2048]{1,0:T(8,128)(2,1)}, bf16[192,2048]{1,0:T(8,128)(2,1)}, u32[]{:S(2)}, u32[]{:S(2)}) collective-permute-start(bf16[192,2048]{1,0:T(8,128)(2,1)} %get-tuple-element.197), channel_id=1, source_target_pairs={{1,0},{3,1},{5,3},{7,5},{6,7},{4,6},{2,4},{0,2},{9,8},{11,9},{13,1... | collective-permute-start | bytes 2359304 | tf_op jit(solution)/shard_map/ppermute | solution.py:797
  409.5 21.2 %collective-permute-start.29 = (bf16[192,2048]{1,0:T(8,128)(2,1)}, bf16[192,2048]{1,0:T(8,128)(2,1)S(1)}, u32[]{:S(2)}, u32[]{:S(2)}) collective-permute-start(bf16[192,2048]{1,0:T(8,128)(2,1)} %get-tuple-element.210), channel_id=1, source_target_pairs={{0,1},{1,3},{3,5},{5,7},{7,6},{6,4},{4,2},{2,0},{8,9},{9,11},{11,1... | collective-permute-start | bytes 2359304 | tf_op jit(solution)/shard_map/ppermute | solution.py:797
  410.9 19.9 %collective-permute-start.30 = (bf16[192,2048]{1,0:T(8,128)(2,1)}, bf16[192,2048]{1,0:T(8,128)(2,1)S(1)}, u32[]{:S(2)}, u32[]{:S(2)}) collective-permute-start(bf16[192,2048]{1,0:T(8,128)(2,1)} %get-tuple-element.211), channel_id=1, source_target_pairs={{1,0},{3,1},{5,3},{7,5},{6,7},{4,6},{2,4},{0,2},{9,8},{11,9},{13,1... | collective-permute-start | bytes 2359304 | tf_op jit(solution)/shard_map/ppermute | solution.py:797
  412.1 18.6 %collective-permute-start.27 = (bf16[48,2048]{1,0:T(8,128)(2,1)S(1)}, bf16[48,2048]{1,0:T(8,128)(2,1)S(1)}, u32[]{:S(2)}, u32[]{:S(2)}) collective-permute-start(bf16[48,2048]{1,0:T(8,128)(2,1)S(1)} %get-tuple-element.231), channel_id=1, source_target_pairs={{0,16},{8,24},{16,0},{24,8},{1,17},{9,25},{17,1},{25,9},{2,18},{10... | collective-permute-start | bytes 589832 | tf_op jit(solution)/shard_map/ppermute | solution.py:734
  (61 other events, 469.3 us)
Sparse Core Ops, SparseCore 0:
  32.2 37.6 all-gather.5
  73.6 26.2 all-gather.9
  105.4 112.8 all-gather.7
  221.8 122.1 reduce-scatter.5
  346.3 42.3 reduce-scatter.3
  391.9 38.6 reduce-scatter.7
